TPU v7x, 512 devices: a whole 4x8x8 slice. The times are simulated.
512 devices in a mesh: feat: 8 (over y), row: 64 (over x, z, core).
Axes of the slice: x: 4, y: 8, z: 8, core: 2. Of those that a mesh axis runs over, the one named last changes fastest.
Arguments:
- bin_values: int32 [131072, 1024], P('row', 'feat'), may hold values from 0 to 127
- leaf_ids: int32 [131072], P('row'), may hold values from 0 to 3
- treated: int32 [131072], P('row'), may hold values 0 or 1
- gradient: bfloat16 [131072], P('row'), may hold values from -6 to 6
- hessian: bfloat16 [131072], P('row'), may hold values from 0.099609375 to 2
Outputs:
- split_gain: float32 [4, 1024, 128], P(None, ('feat', 'row'))
- best_gain: float32 [4], replicated
All inputs are finite; a program needn't handle non-finite values. No bound on the sum of `treated` on one device may be relied on, other than what follows from the above.
Results may differ from a plain program's by a relative error of at most 0.0003.
Values sent between devices are 32-bit elements; how exact they have to be, the bound alone decides.
A program may use at most 64 MiB of HBM per device.

v0:
```python
import math

import jax
import jax.numpy as jnp
from jax import lax
from jax.sharding import PartitionSpec as P

BINS = 128
LEAVES = 4


def arm_stats(leaf_ids, treated, gradient, hessian, leaf_count):
    chosen = treated.astype(jnp.bfloat16)
    others = (1 - treated).astype(jnp.bfloat16)
    columns = jnp.stack(
        [gradient * chosen, hessian * chosen, gradient * others, hessian * others], axis=1
    )
    leaf_hot = (leaf_ids[:, None] == jnp.arange(leaf_count, dtype=jnp.int32)[None, :]).astype(
        jnp.bfloat16
    )
    return (columns[:, :, None] * leaf_hot[:, None, :]).reshape(leaf_ids.shape[0], 4 * leaf_count)


def node_score(totals, leaf_count):
    split_up = totals.reshape(totals.shape[0], 4, leaf_count, totals.shape[2])
    grad_t = split_up[:, 0]
    hess_t = split_up[:, 1]
    grad_c = split_up[:, 2]
    hess_c = split_up[:, 3]
    value_t = grad_t / (hess_t + 1.0)
    value_c = grad_c / (hess_c + 1.0)
    spread = value_t - value_c
    return grad_t * value_t + grad_c * value_c + (hess_t + hess_c) * spread * spread


def body(bin_values, leaf_ids, treated, gradient, hessian):
    row_count, feat_count = bin_values.shape
    bin_count = BINS
    leaf_count = LEAVES
    share_size = feat_count // lax.axis_size("row")
    stat_rows = arm_stats(leaf_ids, treated, gradient, hessian, leaf_count)
    bin_range = jnp.arange(bin_count, dtype=jnp.int32)

    def one_block(feat_block):
        one_hot = (feat_block[:, :, None] == bin_range[None, None, :]).astype(jnp.bfloat16)
        return jnp.einsum("rc,rfb->fcb", stat_rows, one_hot, preferred_element_type=jnp.float32)

    block_width = math.gcd(feat_count, 8)
    blocks = jnp.moveaxis(
        bin_values.reshape(row_count, feat_count // block_width, block_width), 1, 0
    )
    summed = lax.psum(
        lax.map(one_block, blocks).reshape(feat_count, 4 * leaf_count, bin_count), "row"
    )
    owned_rows = lax.dynamic_slice_in_dim(summed, lax.axis_index("row") * share_size, share_size, 0)
    ladder = (bin_range[:, None] <= bin_range[None, :]).astype(jnp.float32)
    left_sums = jnp.einsum("fcb,bk->fck", owned_rows, ladder, precision=lax.Precision.HIGHEST)
    parent_sums = left_sums[:, :, bin_count - 1 :]
    right_sums = parent_sums - left_sums
    gains_local = (
        node_score(left_sums, leaf_count)
        + node_score(right_sums, leaf_count)
        - node_score(parent_sums, leaf_count)
    )
    split_gain = jnp.transpose(gains_local, (1, 0, 2))
    best_gain = lax.pmax(jnp.max(gains_local, axis=(0, 2)), ("feat", "row"))
    return (split_gain, best_gain)


def solution(mesh):
    in_specs = (P("row", "feat"), P("row"), P("row"), P("row"), P("row"))
    out_specs = (P(None, ("feat", "row"), None), P())
    return jax.shard_map(body, mesh=mesh, in_specs=in_specs, out_specs=out_specs, check_vma=False)
```

profile of v0, /device:TPU:1, one launch (start us, length us, event | category | flops | bytes accessed | tf_op | source)
XLA Modules:
  0.0 374.7 jit_solution(13908336219748085189)
XLA Ops:
  7.2 0.0 all-reduce.2.cloned.1.call-start
  7.2 0.8 convert_multiply_fusion.1
  8.1 0.0 copy-start
  8.1 1.6 copy.17
  9.6 0.0 copy-done
  9.7 58.0 %while.11 = (s32[]{:T(128)}, f32[16,8,16,128]{3,2,1,0:T(8,128)}, s32[16,2048,8]{1,2,0:T(8,128)S(1)}, bf16[2048,4]{0,1:T(4,128)(2,1)S(1)}, bf16[2048,4]{0,1:T(4,128)(2,1)S(1)}, /*index=5*/s32[]{:T(128)}) while((s32[]{:T(128)}, f32[16,8,16,128]{3,2,1,0:T(8,128)}, s32[16,2048,8]{1,2,0:T(8,128)S(1)}, bf16[2048,4]{0,1:T(4,128)(2,1)S(1)}, ...), condition=%wide.region_1.2_spmd.clone, body=%wide.region_0.1_spmd.clone.sunk | while | flops 69238784 | bytes 557641 | solution.py:53
  9.8 3.6 fusion.29
  13.5 3.5 fusion.29
  17.1 3.6 fusion.29
  20.7 3.5 fusion.29
  24.3 3.6 fusion.29
  28.0 3.5 fusion.29
  31.6 3.6 fusion.29
  35.2 3.6 fusion.29
  38.8 3.5 fusion.29
  42.5 3.6 fusion.29
  46.1 3.5 fusion.29
  49.7 3.6 fusion.29
  53.3 3.6 fusion.29
  57.0 3.6 fusion.29
  60.6 3.5 fusion.29
  64.2 3.6 fusion.29
  67.8 0.0 all-reduce.2.cloned.1.call-update
  67.8 200.9 %all-reduce.2.cloned.1.call-done = f32[128,16,128]{2,1,0:T(8,128)} async-done(((f32[128,16,128]{2,1,0:T(8,128)}), f32[128,16,128]{2,1,0:T(8,128)}) %all-reduce.2.cloned.1.call-update) | async-done | bytes 1048592 | tf_op jit(solution)/shard_map/psum | solution.py:52
  268.7 0.8 fusion.9
  269.6 0.2 slice_reduce_fusion
  269.8 0.1 reshape.128
  269.8 0.1 broadcast_subtract_fusion
  270.0 0.1 copy.26
  270.1 0.7 fusion.21
  270.7 97.1 %pmax.7 = f32[4]{0:T(128)} all-reduce(f32[4]{0:T(128)S(1)} %get-tuple-element.55), channel_id=1, replica_groups=mesh['feat'=8,'row'=64] {'feat','row'}, use_global_device_ids=true, to_apply=%region_4.5 | all-reduce | flops 4 | bytes 32 | tf_op jit(solution)/shard_map/pmax | solution.py:66
  (58 shorter events, 1.2 us)
Async XLA Ops:
  7.2 261.6 %all-reduce.2.cloned.1.call-start = ((), (), s32[]{:S(2)}) async-start(), calls=%async_computation | async-start | bytes 2097152 | tf_op jit(solution)/shard_map/psum | solution.py:52
  8.1 1.6 copy-start
Sparse Core Ops, SparseCore 0:
  67.9 200.7 all-reduce.1
where the time goes:
time: 375 us
  waiting for transfers between devices  201 us (54%)
  blocking collectives  97.1 us (26%)
  matrix products  57.7 us (15%)
  between operations  14.1 us (4%)
    psum x1, waiting for transfers between devices, body(): lax.psum(lax.map(one_block, blocks).reshape(feat_count, 4 * leaf_count, b...  201 us
    pmax x1, blocking collectives, body(): best_gain = lax.pmax(jnp.max(gains_local, axis=(0, 2)), ('feat', 'row'))  97.1 us
    dot_general x16, matrix products, one_block(): jnp.einsum('rc,rfb->fcb', stat_rows, one_hot, preferred_element_type=jnp....  56.8 us
  transfers between devices with their start and end apart: 1, of which 1 were waited for; matrix products, arithmetic and copies ran while one was open for 0% of the time, Pallas kernels for 0%

commit v1 on v0

v1 whole, which is shorter than its diff:
```python
import jax
import jax.numpy as jnp
from jax import lax
from jax.experimental import pallas as pl
from jax.experimental.pallas import tpu as pltpu
from jax.sharding import PartitionSpec as P

MESH = pl.DeviceIdType.MESH
BF = jnp.bfloat16
NT = (((1,), (1,)), ((), ()))
ROWS = 2048
FEATS = 128
CHUNKS = ROWS // 128
GROUP = 4
NX, NZ, NY = 4, 8, 8


def prepare(bins_ref, leaf_ref, arm_ref, grad_ref, hess_ref, stat_scr, high_scr, low_scr):
    stat = lax.broadcasted_iota(jnp.int32, (16, 128), 0)
    kind, leaf_of = stat // 4, stat % 4
    for c in range(CHUNKS):
        cols = slice(c * 128, (c + 1) * 128)
        grad = grad_ref[c : c + 1, :].astype(jnp.float32)
        hess = hess_ref[c : c + 1, :].astype(jnp.float32)
        keep = (leaf_ref[c : c + 1, :] == leaf_of) & ((arm_ref[c : c + 1, :] == 1) == (kind < 2))
        value = jnp.where(kind % 2 == 0, grad, hess)
        stat_scr[:, cols] = jnp.where(keep, value, 0.0).astype(BF)
    row = lax.broadcasted_iota(jnp.int32, (FEATS, FEATS), 0)
    col = lax.broadcasted_iota(jnp.int32, (FEATS, FEATS), 1)
    eye = (row == col).astype(jnp.float32).astype(BF)
    for c in range(ROWS // 256):
        cols = slice(c * 256, (c + 1) * 256)
        block = bins_ref[cols, :].astype(jnp.float32).astype(BF)
        flipped = lax.dot_general(eye, block, NT, preferred_element_type=jnp.float32)
        high = (flipped >= 64.0).astype(jnp.float32)
        high_scr[:, :, cols] = high.reshape(16, 8, 256)
        low_scr[:, :, cols] = (flipped - high * 64.0).reshape(16, 8, 256)


def hist_kernel(bins_ref, leaf_ref, arm_ref, grad_ref, hess_ref, out_ref, stat_scr, high_scr, low_scr, w_scr, l_scr, a_scr):
    prepare(bins_ref, leaf_ref, arm_ref, grad_ref, hess_ref, stat_scr, high_scr, low_scr)
    sub = lax.broadcasted_iota(jnp.int32, (16, 128), 0)
    lows = [(sub + 16 * k).astype(jnp.float32).astype(BF) for k in range(4)]
    zero = jnp.zeros((16, 128), BF)
    one = jnp.ones((16, 128), BF)
    lane = lax.broadcasted_iota(jnp.int32, (64, 128), 1)
    half = lax.broadcasted_iota(jnp.int32, (32, 128), 1) < 64

    def generate(i, u, slot):
        for j in range(GROUP):
            f = u * GROUP + j
            for c in range(CHUNKS):
                cols = slice(c * 128, (c + 1) * 128)
                high = jnp.broadcast_to(high_scr[i, f : f + 1, cols], (16, 128)).astype(BF)
                low = jnp.broadcast_to(low_scr[i, f : f + 1, cols], (16, 128)).astype(BF)
                stat = stat_scr[:, cols]
                lower = high == zero
                w_scr[slot, 32 * j : 32 * j + 16, cols] = jnp.where(lower, stat, zero)
                w_scr[slot, 32 * j + 16 : 32 * j + 32, cols] = jnp.where(lower, zero, stat)
                for k in range(4):
                    at = 64 * j + 16 * k
                    l_scr[slot, at : at + 16, cols] = jnp.where(low == lows[k], one, zero)

    def multiply(slot):
        a_scr[slot] = lax.dot_general(l_scr[slot], w_scr[slot], NT, preferred_element_type=jnp.float32)

    def extract(g, slot):
        own = a_scr[slot, 0:64, :]
        for j in range(1, GROUP):
            own = jnp.where(lane // 32 == j, a_scr[slot, 64 * j : 64 * (j + 1), :], own)
        top, bottom = own[0:32], own[32:64]
        out_ref[0, g] = jnp.where(half, top, pltpu.roll(bottom, 64, 1))
        out_ref[1, g] = jnp.where(half, pltpu.roll(top, 64, 1), bottom)

    def step(i, carry):
        for u in range(2):
            generate(i, u, u)
            multiply(u)
            extract(2 * i + u, u)
        return carry

    lax.fori_loop(0, FEATS // 8, step, 0)


def finish(block, gain_ref):
    turned = block.T
    lane = lax.broadcasted_iota(jnp.int32, (16, 128), 1)
    best = None
    for j in range(2):
        pieces = [turned[64 * mid + 32 * j + 16 * top : 64 * mid + 32 * j + 16 * top + 16] for top in (0, 1) for mid in (0, 1)]
        left = jnp.concatenate(pieces, axis=1)
        for shift in (1, 2, 4, 8, 16, 32, 64):
            left = left + jnp.where(lane >= shift, pltpu.roll(left, shift, 1), 0.0)
        parent = jnp.broadcast_to(left[:, 127:128], (16, 128))
        gain = score(left) + score(parent - left) - score(parent)
        for leaf in range(4):
            gain_ref[leaf, j : j + 1, :] = gain[leaf : leaf + 1, :]
        best = gain if best is None else jnp.maximum(best, gain)
    top = jnp.max(best, axis=1, keepdims=True)
    return jnp.broadcast_to(jnp.concatenate([top, top], axis=0), (8, 128))


def score(totals):
    grad_t, hess_t, grad_c, hess_c = (totals[4 * k : 4 * k + 4] for k in range(4))
    value_t = grad_t / (hess_t + 1.0)
    value_c = grad_c / (hess_c + 1.0)
    spread = value_t - value_c
    return grad_t * value_t + grad_c * value_c + (hess_t + hess_c) * spread * spread


def exchange_kernel(
    hist_ref, gain_ref, best_ref, core_in, core_sum, x_in, x_sum, z_in, top_out, top_in,
    core_send, core_recv, x_send, x_recv, z_send, z_recv, top_send, top_recv,
):
    feat = lax.axis_index("feat")
    row = lax.axis_index("row")
    core = lax.rem(row, 2)
    z = lax.rem(row // 2, NZ)
    x = row // (2 * NZ)

    def at(x_, z_, core_):
        return (feat, (x_ * NZ + z_) * 2 + core_)

    other = at(x, z, 1 - core)
    x_peer = [at(lax.rem(x + d, NX), z, core) for d in range(NX)]
    x_other = [at(lax.rem(x + d, NX), z, 1 - core) for d in range(NX)]
    z_peer = [at(x, lax.rem(z + d, NZ), core) for d in range(NZ)]
    y_peer = [(lax.rem(feat + d, NY), row) for d in range(NY)]

    barrier = pltpu.get_barrier_semaphore()
    greeted = x_other + x_peer[1:] + z_peer[1:] + y_peer[1:]
    for peer in greeted:
        pl.semaphore_signal(barrier, inc=1, device_id=peer, device_id_type=MESH)
    pl.semaphore_wait(barrier, len(greeted))

    def copy(src, dst, send, recv, peer):
        return pltpu.make_async_remote_copy(
            src_ref=src, dst_ref=dst, send_sem=send, recv_sem=recv, device_id=peer, device_id_type=MESH
        )

    order = [1, 2, 3, 0]
    sent = []
    first = []
    for d in order:
        chips = pl.ds(lax.rem(x + d, NX) * NZ, NZ)
        c = copy(hist_ref.at[1 - core, chips], core_in.at[chips], core_send.at[d], core_recv.at[d], other)
        c.start()
        first.append(c)
    second = []
    for d, c in zip(order, first):
        chips = pl.ds(lax.rem(x + d, NX) * NZ, NZ)
        c.wait_recv()
        core_sum[chips] = hist_ref[core, chips] + core_in[chips]
        if d:
            s = copy(core_sum.at[chips], x_in.at[d - 1], x_send.at[d - 1], x_recv.at[d - 1], x_peer[d])
            s.start()
            second.append(s)
    total = core_sum[pl.ds(x * NZ, NZ)]
    for s in second:
        s.wait_recv()
    x_sum[...] = total + x_in[0] + x_in[1] + x_in[2]
    third = []
    for d in range(1, NZ):
        s = copy(x_sum.at[lax.rem(z + d, NZ)], z_in.at[d - 1], z_send.at[d - 1], z_recv.at[d - 1], z_peer[d])
        s.start()
        third.append(s)
    block = x_sum[z]
    for d, s in enumerate(third):
        s.wait_recv()
        block = block + z_in[d]

    top = finish(block, gain_ref)
    for stage, peers in enumerate((x_other + x_peer[1:], z_peer[1:], y_peer[1:])):
        top_out[stage] = top
        round_ = []
        for k, peer in enumerate(peers):
            s = copy(top_out.at[stage], top_in.at[stage, k], top_send.at[stage, k], top_recv.at[stage, k], peer)
            s.start()
            round_.append(s)
        for k, s in enumerate(round_):
            s.wait_recv()
            top = jnp.maximum(top, top_in[stage, k])
        sent += round_
    for leaf in range(4):
        best_ref[leaf] = jnp.max(top[leaf : leaf + 1, :])
    for s in first + second + third + sent:
        s.wait_send()


def body(bin_values, leaf_ids, treated, gradient, hessian):
    vmem = pl.BlockSpec(memory_space=pltpu.VMEM)
    f32 = jnp.float32
    shape = (CHUNKS, 128)
    hist = pl.pallas_call(
        hist_kernel,
        out_shape=jax.ShapeDtypeStruct((2, 32, 32, 128), f32),
        in_specs=[vmem] * 5,
        out_specs=vmem,
        scratch_shapes=[
            pltpu.VMEM((16, ROWS), BF),
            pltpu.VMEM((16, 8, ROWS), f32),
            pltpu.VMEM((16, 8, ROWS), f32),
            pltpu.VMEM((2, 128, ROWS), BF),
            pltpu.VMEM((2, 256, ROWS), BF),
            pltpu.VMEM((2, 256, 128), f32),
        ],
        compiler_params=pltpu.CompilerParams(vmem_limit_bytes=40 << 20),
    )(bin_values, leaf_ids.reshape(shape), treated.reshape(shape), gradient.reshape(shape), hessian.reshape(shape))
    dma = pltpu.SemaphoreType.DMA
    return pl.pallas_call(
        exchange_kernel,
        out_shape=(jax.ShapeDtypeStruct((4, 2, 128), f32), jax.ShapeDtypeStruct((4,), f32)),
        in_specs=[vmem],
        out_specs=(vmem, pl.BlockSpec(memory_space=pltpu.SMEM)),
        scratch_shapes=[
            pltpu.VMEM((32, 32, 128), f32),
            pltpu.VMEM((32, 32, 128), f32),
            pltpu.VMEM((NX - 1, NZ, 32, 128), f32),
            pltpu.VMEM((NZ, 32, 128), f32),
            pltpu.VMEM((NZ - 1, 32, 128), f32),
            pltpu.VMEM((3, 8, 128), f32),
            pltpu.VMEM((3, 7, 8, 128), f32),
            dma((4,)), dma((4,)), dma((3,)), dma((3,)), dma((7,)), dma((7,)), dma((3, 7)), dma((3, 7)),
        ],
        compiler_params=pltpu.CompilerParams(
            collective_id=0, has_side_effects=True, vmem_limit_bytes=20 << 20
        ),
    )(hist)


def solution(mesh):
    in_specs = (P("row", "feat"), P("row"), P("row"), P("row"), P("row"))
    out_specs = (P(None, ("feat", "row"), None), P())
    return jax.shard_map(body, mesh=mesh, in_specs=in_specs, out_specs=out_specs, check_vma=False)
```

time: 375 us -> 65.9 us (0.18)
  waiting for transfers between devices: 201 us -> 0 us
  blocking collectives: 97.1 us -> 0 us
  Pallas kernels: 0 us -> 59.8 us
  matrix products: 57.7 us -> 0 us
  between operations: 14.1 us -> 0.66 us
    psum x1 -> x0, waiting for transfers between devices: 201 us -> none  [body(): lax.psum(lax.map(one_block, blocks).reshape(feat_count, 4 * leaf_count, b...]
    pmax x1 -> x0, blocking collectives: 97.1 us -> none  [body(): best_gain = lax.pmax(jnp.max(gains_local, axis=(0, 2)), ('feat', 'row'))]
    pallas_call x0 -> x2, Pallas kernels: none -> 59.8 us  [the longest x1 43.9 us: body(): pl.pallas_call(exchange_kernel, out_shape=(jax.ShapeDtypeStruct((4, 2, 12...]
    dot_general x17 -> x0, matrix products: 57.7 us -> none  [the longest x16 56.8 us: one_block(): jnp.einsum('rc,rfb->fcb', stat_rows, one_hot, preferred_element_type=jnp....]
  transfers between devices with their start and end apart: 1 -> 0, of which waited for: 1 -> 0; matrix products, arithmetic and copies ran while one was open for 0% -> 0% of each run, Pallas kernels for 0% -> 0%
where the time goes in v1:
time: 65.9 us; the launch traced here: 65.6 us
  Pallas kernels  59.8 us (91%)
  local copies, waits for them, and re-layouts  5.09 us (8%)
  between operations  0.66 us (1%)
    pallas_call x1, Pallas kernels, body(): pl.pallas_call(exchange_kernel, out_shape=(jax.ShapeDtypeStruct((4, 2, 12...  43.9 us
    pallas_call x1, Pallas kernels, body(): pl.pallas_call(hist_kernel, out_shape=jax.ShapeDtypeStruct((2, 32, 32, 12...  16 us
    unnamed x12, local copies, waits for them, and re-layouts  5.09 us

profile of v1, /device:TPU:1, one launch (start us, length us, event | category | flops | bytes accessed | tf_op | source)
XLA Modules:
  0.0 65.6 jit_solution(2589309237067980484)
XLA Ops:
  0.6 0.0 copy-start.3
  0.6 0.7 %copy-done.3 = bf16[2048]{0:T(1024)(128)(2,1)S(1)} copy-done((bf16[2048]{0:T(1024)(128)(2,1)S(1)}, bf16[2048]{0:T(1024)(128)(2,1)}, u32[]{:S(2)}) %copy-start.3) | copy-done | bytes 4120
  1.3 0.0 copy-start
  1.3 1.2 %copy-done = s32[2048,128]{1,0:T(8,128)S(1)} copy-done((s32[2048,128]{1,0:T(8,128)S(1)}, s32[2048,128]{1,0:T(8,128)}, u32[]{:S(2)}) %copy-start) | copy-done | bytes 1048600
  2.5 0.0 copy-start.1
  2.5 0.7 %copy-done.1 = s32[2048]{0:T(1024)S(1)} copy-done((s32[2048]{0:T(1024)S(1)}, s32[2048]{0:T(1024)}, u32[]{:S(2)}) %copy-start.1) | copy-done | bytes 8216
  3.2 0.0 copy-start.2
  3.2 0.7 %copy-done.2 = s32[2048]{0:T(1024)S(1)} copy-done((s32[2048]{0:T(1024)S(1)}, s32[2048]{0:T(1024)}, u32[]{:S(2)}) %copy-start.2) | copy-done | bytes 8216
  3.9 0.0 copy-start.4
  3.9 0.7 %copy-done.4 = bf16[2048]{0:T(1024)(128)(2,1)S(1)} copy-done((bf16[2048]{0:T(1024)(128)(2,1)S(1)}, bf16[2048]{0:T(1024)(128)(2,1)}, u32[]{:S(2)}) %copy-start.4) | copy-done | bytes 4120
  4.6 16.0 %shard_map.68.hist_ref = f32[2,32,32,128]{3,2,1,0:T(8,128)S(1)} custom-call(s32[2048,128]{1,0:T(8,128)S(1)} %copy-done, s32[16,128]{1,0:T(8,128)S(1)} %bitcast.4, s32[16,128]{1,0:T(8,128)S(1)} %bitcast.5, bf16[16,128]{1,0:T(8,128)(2,1)S(1)} %bitcast.6, bf16[16,128]{1,0:T(8,128)(2,1)S(1)} %bitcast.7), custom_call_target="tpu_custom_call" | custom-call | tf_op jit(solution)/shard_map/pallas_call | solution.py:194
  20.6 43.9 %shard_map.69 = (f32[4,2,128]{2,1,0:T(2,128)S(1)}, f32[4]{0:T(128)S(1)}) custom-call(f32[2,32,32,128]{3,2,1,0:T(8,128)S(1)} %shard_map.68.hist_ref), custom_call_target="tpu_custom_call" | custom-call | tf_op jit(solution)/shard_map/pallas_call | solution.py:210
  64.5 0.6 copy.9
  65.1 0.5 copy.10
Async XLA Ops:
  0.6 0.7 %copy-start.3 = (bf16[2048]{0:T(1024)(128)(2,1)S(1)}, bf16[2048]{0:T(1024)(128)(2,1)}, u32[]{:S(2)}) copy-start(bf16[2048]{0:T(1024)(128)(2,1)} %param.8) | copy-start | bytes 12292
  1.3 1.2 %copy-start = (s32[2048,128]{1,0:T(8,128)S(1)}, s32[2048,128]{1,0:T(8,128)}, u32[]{:S(2)}) copy-start(s32[2048,128]{1,0:T(8,128)} %bins_ref.1) | copy-start | bytes 3145732
  2.5 0.7 %copy-start.1 = (s32[2048]{0:T(1024)S(1)}, s32[2048]{0:T(1024)}, u32[]{:S(2)}) copy-start(s32[2048]{0:T(1024)} %param.6) | copy-start | bytes 24580
  3.2 0.7 %copy-start.2 = (s32[2048]{0:T(1024)S(1)}, s32[2048]{0:T(1024)}, u32[]{:S(2)}) copy-start(s32[2048]{0:T(1024)} %param.7) | copy-start | bytes 24580
  3.9 0.7 %copy-start.4 = (bf16[2048]{0:T(1024)(128)(2,1)S(1)}, bf16[2048]{0:T(1024)(128)(2,1)}, u32[]{:S(2)}) copy-start(bf16[2048]{0:T(1024)(128)(2,1)} %param.9) | copy-start | bytes 12292

commit v2 on v1

v2 whole, which is shorter than its diff:
```python
import jax
import jax.numpy as jnp
from jax import lax
from jax.experimental import pallas as pl
from jax.experimental.pallas import tpu as pltpu
from jax.sharding import PartitionSpec as P

MESH = pl.DeviceIdType.MESH
BF = jnp.bfloat16
NT = (((1,), (1,)), ((), ()))
ROWS = 2048
FEATS = 128
CHUNKS = ROWS // 128
GROUP = 4
NX, NZ, NY = 4, 8, 8
FAR = ((4, 3), (5, 2), (6, 1), (7, 0))


def prepare(bins_ref, leaf_ref, arm_ref, grad_ref, hess_ref, stat_scr, high_scr, low_scr):
    stat = lax.broadcasted_iota(jnp.int32, (16, 128), 0)
    kind, leaf_of = stat // 4, stat % 4
    for c in range(CHUNKS):
        cols = slice(c * 128, (c + 1) * 128)
        grad = grad_ref[c : c + 1, :].astype(jnp.float32)
        hess = hess_ref[c : c + 1, :].astype(jnp.float32)
        keep = (leaf_ref[c : c + 1, :] == leaf_of) & ((arm_ref[c : c + 1, :] == 1) == (kind < 2))
        value = jnp.where(kind % 2 == 0, grad, hess)
        stat_scr[:, cols] = jnp.where(keep, value, 0.0).astype(BF)
    row = lax.broadcasted_iota(jnp.int32, (2 * FEATS, FEATS), 0)
    col = lax.broadcasted_iota(jnp.int32, (2 * FEATS, FEATS), 1)
    pick = ((row // 8 * 4 + row % 8 == col) & (row % 8 < 4)).astype(jnp.float32).astype(BF)
    for c in range(ROWS // 256):
        cols = slice(c * 256, (c + 1) * 256)
        block = bins_ref[cols, :].astype(jnp.float32).astype(BF)
        flipped = lax.dot_general(pick, block, NT, preferred_element_type=jnp.float32)
        high = (flipped >= 64.0).astype(jnp.float32)
        high_scr[:, :, cols] = high.reshape(32, 8, 256)
        low_scr[:, :, cols] = (flipped - high * 64.0).reshape(32, 8, 256)


def make_histogram(hist, stat_scr, high_scr, low_scr, w_scr, l_scr, a_scr):
    sub = lax.broadcasted_iota(jnp.int32, (16, 128), 0)
    lows = [(sub + 16 * k).astype(jnp.float32).astype(BF) for k in range(4)]
    zero = jnp.zeros((16, 128), BF)
    one = jnp.ones((16, 128), BF)
    lane = lax.broadcasted_iota(jnp.int32, (64, 128), 1)
    half = lax.broadcasted_iota(jnp.int32, (32, 128), 1) < 64

    def generate(chip, slot):
        for j in range(GROUP):
            for c in range(CHUNKS):
                cols = slice(c * 128, (c + 1) * 128)
                high = jnp.broadcast_to(high_scr[chip, j : j + 1, cols], (16, 128)).astype(BF)
                low = jnp.broadcast_to(low_scr[chip, j : j + 1, cols], (16, 128)).astype(BF)
                stat = stat_scr[:, cols]
                lower = high == zero
                w_scr[slot, 32 * j : 32 * j + 16, cols] = jnp.where(lower, stat, zero)
                w_scr[slot, 32 * j + 16 : 32 * j + 32, cols] = jnp.where(lower, zero, stat)
                for k in range(4):
                    at = 64 * j + 16 * k
                    l_scr[slot, at : at + 16, cols] = jnp.where(low == lows[k], one, zero)

    def multiply(slot):
        a_scr[slot] = lax.dot_general(l_scr[slot], w_scr[slot], NT, preferred_element_type=jnp.float32)

    def extract(chunk, u, i, slot):
        own = a_scr[slot, 0:64, :]
        for j in range(1, GROUP):
            own = jnp.where(lane // 32 == j, a_scr[slot, 64 * j : 64 * (j + 1), :], own)
        top, bottom = own[0:32], own[32:64]
        hist[0, chunk, u, i] = jnp.where(half, top, pltpu.roll(bottom, 64, 1))
        hist[1, chunk, u, i] = jnp.where(half, pltpu.roll(top, 64, 1), bottom)

    def one_chunk(chunk, far):
        def step(i, carry):
            for u in range(2):
                generate(i * NZ + far[u], u)
                multiply(u)
                extract(chunk, u, i, u)
            return carry

        lax.fori_loop(0, NX, step, 0)

    return one_chunk


def finish(block, gain_ref):
    turned = block.T
    lane = lax.broadcasted_iota(jnp.int32, (16, 128), 1)
    best = None
    for j in range(2):
        pieces = [turned[64 * mid + 32 * j + 16 * top : 64 * mid + 32 * j + 16 * top + 16] for top in (0, 1) for mid in (0, 1)]
        left = jnp.concatenate(pieces, axis=1)
        for shift in (1, 2, 4, 8, 16, 32, 64):
            left = left + jnp.where(lane >= shift, pltpu.roll(left, shift, 1), 0.0)
        parent = jnp.broadcast_to(left[:, 127:128], (16, 128))
        gain = score(left) + score(parent - left) - score(parent)
        for leaf in range(4):
            gain_ref[leaf, j : j + 1, :] = gain[leaf : leaf + 1, :]
        best = gain if best is None else jnp.maximum(best, gain)
    top = jnp.max(best, axis=1, keepdims=True)
    return jnp.broadcast_to(jnp.concatenate([top, top], axis=0), (8, 128))


def score(totals):
    grad_t, hess_t, grad_c, hess_c = (totals[4 * k : 4 * k + 4] for k in range(4))
    value_t = grad_t / (hess_t + 1.0)
    value_c = grad_c / (hess_c + 1.0)
    spread = value_t - value_c
    return grad_t * value_t + grad_c * value_c + (hess_t + hess_c) * spread * spread


def kernel(
    bins_hbm, leaf_hbm, arm_hbm, grad_hbm, hess_hbm, gain_ref, best_ref,
    bins_ref, leaf_ref, arm_ref, grad_ref, hess_ref, stat_scr, high_scr, low_scr, w_scr, l_scr, a_scr,
    hist, core_in, core_sum, x_in, x_sum, z_in, top_out, top_in,
    load_sem, core_send, core_recv, x_send, x_recv, z_send, z_recv, top_send, top_recv,
):
    feat = lax.axis_index("feat")
    row = lax.axis_index("row")
    core = lax.rem(row, 2)
    z = lax.rem(row // 2, NZ)
    x = row // (2 * NZ)

    def at(x_, z_, core_):
        return (feat, (x_ * NZ + z_) * 2 + core_)

    other = at(x, z, 1 - core)
    x_peer = [at(lax.rem(x + d, NX), z, core) for d in range(NX)]
    z_peer = [at(x, lax.rem(z + d, NZ), core) for d in range(NZ)]
    y_peer = [(lax.rem(feat + d, NY), row) for d in range(NY)]

    loads = [
        pltpu.make_async_copy(src, dst, load_sem.at[k])
        for k, (src, dst) in enumerate(
            zip(
                (leaf_hbm, arm_hbm, grad_hbm, hess_hbm, bins_hbm),
                (leaf_ref, arm_ref, grad_ref, hess_ref, bins_ref),
            )
        )
    ]
    for load in loads:
        load.start()
    barrier = pltpu.get_barrier_semaphore()
    greeted = [other] + x_peer[1:] + z_peer[1:] + y_peer[1:]
    for peer in greeted:
        pl.semaphore_signal(barrier, inc=1, device_id=peer, device_id_type=MESH)
    for load in loads:
        load.wait()

    prepare(bins_ref, leaf_ref, arm_ref, grad_ref, hess_ref, stat_scr, high_scr, low_scr)
    one_chunk = make_histogram(hist, stat_scr, high_scr, low_scr, w_scr, l_scr, a_scr)

    def copy(src, dst, send, recv, peer):
        return pltpu.make_async_remote_copy(
            src_ref=src, dst_ref=dst, send_sem=send, recv_sem=recv, device_id=peer, device_id_type=MESH
        )

    core_copies, x_copies, z_copies, top_copies = [], {}, {}, []

    def start_core(c):
        s = copy(hist.at[1 - core, c], core_in.at[c], core_send.at[c], core_recv.at[c], other)
        s.start()
        core_copies.append(s)

    def start_x(c):
        core_copies[c].wait_recv()
        core_sum[c] = hist[core, c] + core_in[c]
        for d in (2, 1, 3):
            s = copy(
                core_sum.at[c, :, lax.rem(x + d, NX)], x_in.at[c, d - 1], x_send.at[c, d - 1], x_recv.at[c, d - 1], x_peer[d]
            )
            s.start()
            x_copies[c, d] = s

    def start_z(c):
        for d in (1, 3, 2):
            x_copies[c, d].wait_recv()
        x_sum[c] = core_sum[c, :, x] + x_in[c, 0] + x_in[c, 1] + x_in[c, 2]
        for u, d in enumerate(FAR[c]):
            if d:
                s = copy(x_sum.at[c, u], z_in.at[d - 1], z_send.at[d - 1], z_recv.at[d - 1], z_peer[d])
                s.start()
                z_copies[d] = s

    for c in range(4):
        one_chunk(c, [lax.rem(z + d, NZ) for d in FAR[c]])
        if c == 0:
            pl.semaphore_wait(barrier, len(greeted))
        start_core(c)
        if c >= 1:
            start_x(c - 1)
        if c >= 2:
            start_z(c - 2)
    start_x(3)
    start_z(2)
    start_z(3)
    block = x_sum[3, 1]
    for d in (1, 7, 2, 6, 3, 5, 4):
        z_copies[d].wait_recv()
        block = block + z_in[d - 1]

    top = finish(block, gain_ref)
    for stage, peers in enumerate(([other], x_peer[1:], z_peer[1:], y_peer[1:])):
        top_out[stage] = top
        round_ = []
        for k, peer in enumerate(peers):
            s = copy(top_out.at[stage], top_in.at[stage, k], top_send.at[stage, k], top_recv.at[stage, k], peer)
            s.start()
            round_.append(s)
        for k, s in enumerate(round_):
            s.wait_recv()
            top = jnp.maximum(top, top_in[stage, k])
        top_copies += round_
    for leaf in range(4):
        best_ref[leaf] = jnp.max(top[leaf : leaf + 1, :])
    for s in core_copies + list(x_copies.values()) + list(z_copies.values()) + top_copies:
        s.wait_send()


def body(bin_values, leaf_ids, treated, gradient, hessian):
    vmem = pl.BlockSpec(memory_space=pltpu.VMEM)
    f32 = jnp.float32
    shape = (CHUNKS, 128)
    dma = pltpu.SemaphoreType.DMA
    return pl.pallas_call(
        kernel,
        out_shape=(jax.ShapeDtypeStruct((4, 2, 128), f32), jax.ShapeDtypeStruct((4,), f32)),
        in_specs=[pl.BlockSpec(memory_space=pltpu.HBM)] * 5,
        out_specs=(vmem, pl.BlockSpec(memory_space=pltpu.SMEM)),
        scratch_shapes=[
            pltpu.VMEM((ROWS, FEATS), jnp.int32),
            pltpu.VMEM(shape, jnp.int32),
            pltpu.VMEM(shape, jnp.int32),
            pltpu.VMEM(shape, BF),
            pltpu.VMEM(shape, BF),
            pltpu.VMEM((16, ROWS), BF),
            pltpu.VMEM((32, 8, ROWS), f32),
            pltpu.VMEM((32, 8, ROWS), f32),
            pltpu.VMEM((2, 128, ROWS), BF),
            pltpu.VMEM((2, 256, ROWS), BF),
            pltpu.VMEM((2, 256, 128), f32),
            pltpu.VMEM((2, 4, 2, NX, 32, 128), f32),
            pltpu.VMEM((4, 2, NX, 32, 128), f32),
            pltpu.VMEM((4, 2, NX, 32, 128), f32),
            pltpu.VMEM((4, NX - 1, 2, 32, 128), f32),
            pltpu.VMEM((4, 2, 32, 128), f32),
            pltpu.VMEM((NZ - 1, 32, 128), f32),
            pltpu.VMEM((4, 8, 128), f32),
            pltpu.VMEM((4, 7, 8, 128), f32),
            dma((5,)), dma((4,)), dma((4,)), dma((4, 3)), dma((4, 3)), dma((7,)), dma((7,)), dma((4, 7)), dma((4, 7)),
        ],
        compiler_params=pltpu.CompilerParams(collective_id=0, has_side_effects=True, vmem_limit_bytes=24 << 20),
    )(bin_values, leaf_ids.reshape(shape), treated.reshape(shape), gradient.reshape(shape), hessian.reshape(shape))


def solution(mesh):
    in_specs = (P("row", "feat"), P("row"), P("row"), P("row"), P("row"))
    out_specs = (P(None, ("feat", "row"), None), P())
    return jax.shard_map(body, mesh=mesh, in_specs=in_specs, out_specs=out_specs, check_vma=False)
```

time: 65.9 us -> 56.9 us (0.86)
  Pallas kernels: 59.8 us -> 50.8 us
    pallas_call x2 -> x1, Pallas kernels: 59.8 us -> 50.8 us  [body(): pl.pallas_call(kernel, out_shape=(jax.ShapeDtypeStruct((4, 2, 128), f32),...]
where the time goes in v2:
time: 56.9 us; the launch traced here: 56.5 us
  Pallas kernels  50.8 us (89%)
  local copies, waits for them, and re-layouts  5.09 us (9%)
  between operations  0.65 us (1%)
    pallas_call x1, Pallas kernels, body(): pl.pallas_call(kernel, out_shape=(jax.ShapeDtypeStruct((4, 2, 128), f32),...  50.8 us
    unnamed x12, local copies, waits for them, and re-layouts  5.09 us

profile of v2, /device:TPU:1, one launch (start us, length us, event | category | flops | bytes accessed | tf_op | source)
XLA Modules:
  0.0 56.5 jit_solution(8960683653152246095)
XLA Ops:
  0.6 0.0 copy-start.3
  0.6 0.7 %copy-done.3 = bf16[2048]{0:T(1024)(128)(2,1)S(1)} copy-done((bf16[2048]{0:T(1024)(128)(2,1)S(1)}, bf16[2048]{0:T(1024)(128)(2,1)}, u32[]{:S(2)}) %copy-start.3) | copy-done | bytes 4120
  1.3 0.0 copy-start
  1.3 1.2 %copy-done = s32[2048,128]{1,0:T(8,128)S(1)} copy-done((s32[2048,128]{1,0:T(8,128)S(1)}, s32[2048,128]{1,0:T(8,128)}, u32[]{:S(2)}) %copy-start) | copy-done | bytes 1048600
  2.5 0.0 copy-start.1
  2.5 0.7 %copy-done.1 = s32[2048]{0:T(1024)S(1)} copy-done((s32[2048]{0:T(1024)S(1)}, s32[2048]{0:T(1024)}, u32[]{:S(2)}) %copy-start.1) | copy-done | bytes 8216
  3.2 0.0 copy-start.2
  3.2 0.7 %copy-done.2 = s32[2048]{0:T(1024)S(1)} copy-done((s32[2048]{0:T(1024)S(1)}, s32[2048]{0:T(1024)}, u32[]{:S(2)}) %copy-start.2) | copy-done | bytes 8216
  3.9 0.0 copy-start.4
  3.9 0.7 %copy-done.4 = bf16[2048]{0:T(1024)(128)(2,1)S(1)} copy-done((bf16[2048]{0:T(1024)(128)(2,1)S(1)}, bf16[2048]{0:T(1024)(128)(2,1)}, u32[]{:S(2)}) %copy-start.4) | copy-done | bytes 4120
  4.6 50.8 %shard_map.68 = (f32[4,2,128]{2,1,0:T(2,128)S(1)}, f32[4]{0:T(128)S(1)}) custom-call(s32[2048,128]{1,0:T(8,128)S(1)} %copy-done, s32[16,128]{1,0:T(8,128)S(1)} %bitcast.4, s32[16,128]{1,0:T(8,128)S(1)} %bitcast.5, bf16[16,128]{1,0:T(8,128)(2,1)S(1)} %bitcast.6, bf16[16,128]{1,0:T(8,128)(2,1)S(1)} %bitcast.7), custom_call_target="tpu_custom_call" | custom-call | tf_op jit(solution)/shard_map/pallas_call | solution.py:226
  55.4 0.6 %copy.9 = f32[4,2,128]{2,1,0:T(2,128)} copy(f32[4,2,128]{2,1,0:T(2,128)S(1)} %get-tuple-element.4) | data formatting | bytes 8192
  56.0 0.5 copy.10
Async XLA Ops:
  0.6 0.7 %copy-start.3 = (bf16[2048]{0:T(1024)(128)(2,1)S(1)}, bf16[2048]{0:T(1024)(128)(2,1)}, u32[]{:S(2)}) copy-start(bf16[2048]{0:T(1024)(128)(2,1)} %param.8) | copy-start | bytes 12292
  1.3 1.2 %copy-start = (s32[2048,128]{1,0:T(8,128)S(1)}, s32[2048,128]{1,0:T(8,128)}, u32[]{:S(2)}) copy-start(s32[2048,128]{1,0:T(8,128)} %bins_hbm.1) | copy-start | bytes 3145732
  2.5 0.7 %copy-start.1 = (s32[2048]{0:T(1024)S(1)}, s32[2048]{0:T(1024)}, u32[]{:S(2)}) copy-start(s32[2048]{0:T(1024)} %param.6) | copy-start | bytes 24580
  3.2 0.7 %copy-start.2 = (s32[2048]{0:T(1024)S(1)}, s32[2048]{0:T(1024)}, u32[]{:S(2)}) copy-start(s32[2048]{0:T(1024)} %param.7) | copy-start | bytes 24580
  3.9 0.7 %copy-start.4 = (bf16[2048]{0:T(1024)(128)(2,1)S(1)}, bf16[2048]{0:T(1024)(128)(2,1)}, u32[]{:S(2)}) copy-start(bf16[2048]{0:T(1024)(128)(2,1)} %param.9) | copy-start | bytes 12292

commit v3 on v0

v3 whole, which is shorter than its diff:
```python
import jax
import jax.numpy as jnp
from jax import lax
from jax.experimental import pallas as pl
from jax.experimental.pallas import tpu as pltpu
from jax.sharding import PartitionSpec as P

MESH = pl.DeviceIdType.MESH
BF = jnp.bfloat16
F32 = jnp.float32
ROWS = 2048
FEATS = 128
TILE = 256
TILES = ROWS // TILE
PAIRS = 8
NX, NZ, NY = 4, 8, 8


def load_stats(leaf_ref, arm_ref, grad_ref, hess_ref, stat_scr):
    stat = lax.broadcasted_iota(jnp.int32, (16, 128), 0)
    kind, leaf_of = stat // 4, stat % 4
    for c in range(ROWS // 128):
        grad = grad_ref[c : c + 1, :].astype(F32)
        hess = hess_ref[c : c + 1, :].astype(F32)
        keep = (leaf_ref[c : c + 1, :] == leaf_of) & ((arm_ref[c : c + 1, :] == 1) == (kind < 2))
        value = jnp.where(kind % 2 == 0, grad, hess)
        stat_scr[:, c * 128 : (c + 1) * 128] = jnp.where(keep, value, 0.0).astype(BF)


def lane_orders(z):
    feat = lax.broadcasted_iota(jnp.int32, (TILE, 128), 0)
    lane = lax.broadcasted_iota(jnp.int32, (TILE, 128), 1)
    owner = lane // 8
    core, u, x = owner // 8, owner // 4 % 2, owner % 4
    orders = []
    for c in range(4):
        far = lax.rem(z + jnp.where(u == 0, 4 + c, 3 - c), NZ)
        orders.append((feat == ((x * NZ + far) * 2 + core) * 2 + lane % 2).astype(F32).astype(BF))
    return [jnp.concatenate(orders[:2], axis=1), jnp.concatenate(orders[2:], axis=1)]


def spread_bins(accs, orders, bins_ref, bins_scr):
    def drain(r):
        rows = slice(r * TILE, (r + 1) * TILE)
        for p in range(2):
            spread = pltpu.matmul_pop(accs[2 * (r % 2) + p]).astype(BF)
            bins_scr[2 * p, rows, :] = spread[:, :128]
            bins_scr[2 * p + 1, rows, :] = spread[:, 128:]

    for p in range(2):
        pltpu.matmul_push_rhs(orders[p], staging_register=0, mxu_index=p)
    for r in range(TILES):
        block = bins_ref[r * TILE : (r + 1) * TILE, :].astype(F32).astype(BF)
        block = jnp.concatenate([block, block], axis=1)
        for p in range(2):
            pltpu.matmul_acc_lhs(accs[2 * (r % 2) + p], block, load_staged_rhs=0 if r == 0 else None)
        if r:
            drain(r - 1)
    drain(TILES - 1)


def half_chunk(accs, c, w, stat_scr, bins_scr, turn_scr):
    shape = (16, 16, 128)
    one, zero = jnp.ones(shape, BF), jnp.zeros(shape, BF)
    group = lax.broadcasted_iota(jnp.int32, (16, 128), 1) % 8 // 2
    first = 2 * PAIRS * w
    wanted = [(group * 32 + (first + q)).astype(F32).astype(BF)[None] for q in range(2 * PAIRS)]
    for k in range(TILES):
        rows = slice(k * TILE, (k + 1) * TILE)
        bins = bins_scr[c, rows, :].reshape(shape)
        stat = stat_scr[:, rows]
        for q in range(PAIRS):
            hot = [jnp.where(bins == wanted[2 * q + e], one, zero).reshape(TILE, 128) for e in range(2)]
            reg = (k * (PAIRS // 2) + q // 2) % 2
            pltpu.matmul_push_rhs(jnp.concatenate(hot, axis=1), staging_register=reg, mxu_index=q % 2)
            pltpu.matmul_acc_lhs(accs[q], stat, load_staged_rhs=reg)
    for q in range(PAIRS):
        sums = pltpu.matmul_pop(accs[q])
        for e in range(2):
            turn_scr[pl.ds(first + 2 * q + e, 16, stride=32), :] = sums[:, e * 128 : (e + 1) * 128]


def turn_chunk(c, turn_scr, hist):
    for t in range(4):
        turned = turn_scr[t * 128 : (t + 1) * 128, :].T
        hist[c, :, :, :, :, t * 128 : (t + 1) * 128] = turned.reshape(2, 2, NX, 8, 128)


def score(totals):
    grad_t, hess_t, grad_c, hess_c = (totals[8 * k : 8 * k + 8] for k in range(4))
    value_t = grad_t / (hess_t + 1.0)
    value_c = grad_c / (hess_c + 1.0)
    spread = value_t - value_c
    return grad_t * value_t + grad_c * value_c + (hess_t + hess_c) * spread * spread


def finish(block, gain_ref):
    x = jnp.concatenate([block[:, 128 * k : 128 * (k + 1)] for k in range(4)], axis=0)
    low = lax.broadcasted_iota(jnp.int32, (32, 128), 1) % 32
    sub = lax.broadcasted_iota(jnp.int32, (32, 128), 0) % 8
    for shift in (1, 2, 4, 8, 16):
        x = x + jnp.where(low >= shift, pltpu.roll(x, shift, 1), 0.0)
    total = jnp.where(low == 31, x, 0.0)
    for shift in (1, 2, 4, 8, 16):
        total = total + jnp.where(low <= 31 - shift, pltpu.roll(total, 128 - shift, 1), 0.0)
    upto = total + jnp.where(sub >= 2, pltpu.roll(total, 2, 0), 0.0)
    upto = upto + jnp.where(sub >= 4, pltpu.roll(upto, 4, 0), 0.0)
    left = x + jnp.where(sub >= 2, pltpu.roll(upto, 2, 0), 0.0)
    parent = jnp.where(sub >= 6, upto, 0.0)
    parent = parent + jnp.where((sub >= 4) & (sub < 6), pltpu.roll(parent, 30, 0), 0.0)
    parent = parent + jnp.where(sub < 4, pltpu.roll(parent, 28, 0), 0.0)
    gain = score(left) + score(parent - left) - score(parent)
    lane_block = lax.broadcasted_iota(jnp.int32, (8, 128), 1) // 32
    row_block = lax.broadcasted_iota(jnp.int32, (8, 128), 0) // 2
    out = gain
    for d in range(1, 4):
        moved = pltpu.roll(pltpu.roll(gain, 32 * d, 1), 8 - 2 * d, 0)
        out = jnp.where((lane_block + 4 - row_block) % 4 == d, moved, out)
    gain_ref[...] = out
    return jnp.max(gain, axis=0, keepdims=True)


def kernel(
    bins_hbm, leaf_hbm, arm_hbm, grad_hbm, hess_hbm, gain_ref, best_ref,
    bins_ref, leaf_ref, arm_ref, grad_ref, hess_ref, stat_scr, bins_scr, turn_scr,
    hist, core_in, core_sum, x_in, x_sum, z_in, last_x, last_z, top_out, top_in,
    load_sem, core_send, core_recv, x_send, x_recv, z_send, z_recv,
    last_x_send, last_x_recv, last_z_send, last_z_recv, top_send, top_recv,
):
    feat = lax.axis_index("feat")
    row = lax.axis_index("row")
    core = lax.rem(row, 2)
    z = lax.rem(row // 2, NZ)
    x = row // (2 * NZ)

    def at(dx, dz, core_):
        return (feat, (lax.rem(x + dx, NX) * NZ + lax.rem(z + dz, NZ)) * 2 + core_)

    other = at(0, 0, 1 - core)
    x_peer = [at(d, 0, core) for d in range(NX)]
    y_peer = [(lax.rem(feat + d, NY), row) for d in range(NY)]

    loads = [
        pltpu.make_async_copy(src, dst, load_sem.at[k])
        for k, (src, dst) in enumerate(
            zip(
                (leaf_hbm, arm_hbm, grad_hbm, hess_hbm, bins_hbm),
                (leaf_ref, arm_ref, grad_ref, hess_ref, bins_ref),
            )
        )
    ]
    for load in loads:
        load.start()
    barrier = pltpu.get_barrier_semaphore()
    greeted = [other] + x_peer[1:] + [at(0, d, core) for d in range(1, NZ)] + y_peer[1:]
    greeted += [at(d, e, core) for d in range(1, NX) for e in (1, NZ - 1)]
    for peer in greeted:
        pl.semaphore_signal(barrier, inc=1, device_id=peer, device_id_type=MESH)

    for load in loads[:4]:
        load.wait()
    load_stats(leaf_ref, arm_ref, grad_ref, hess_ref, stat_scr)
    orders = lane_orders(z)
    loads[4].wait()
    pl.run_scoped(
        lambda *accs: spread_bins(accs, orders, bins_ref, bins_scr),
        *[pltpu.ACC(q % 2)((TILE, TILE), F32) for q in range(4)],
    )

    def copy(src, dst, send, recv, peer):
        return pltpu.make_async_remote_copy(
            src_ref=src, dst_ref=dst, send_sem=send, recv_sem=recv, device_id=peer, device_id_type=MESH
        )

    def core_copy(c):
        return copy(hist.at[c, 1 - core], core_in.at[c], core_send.at[c], core_recv.at[c], other)

    def x_copy(c, d):
        return copy(
            core_sum.at[c, :, lax.rem(x + d, NX)], x_in.at[c, d - 1], x_send.at[c, d - 1], x_recv.at[c, d - 1], x_peer[d]
        )

    def z_copy(c, u):
        d = 3 - c if u else 4 + c
        return copy(x_sum.at[c, u], z_in.at[d - 1], z_send.at[d - 1], z_recv.at[d - 1], at(0, d, core))

    def last_x_copy(d):
        return copy(
            core_sum.at[3, 1, lax.rem(x + d, NX)], last_x.at[d - 1], last_x_send.at[d - 1], last_x_recv.at[d - 1], x_peer[d]
        )

    def last_z_copy(d):
        return copy(
            core_sum.at[3, 0, lax.rem(x + d, NX)], last_z.at[d], last_z_send.at[d], last_z_recv.at[d], at(d, NZ - 1, core)
        )

    def add_core(c):
        core_copy(c).wait_recv()
        core_sum[c] = hist[c, core] + core_in[c]

    def start_x(c):
        add_core(c)
        for d in (2, 1, 3):
            x_copy(c, d).start()

    def start_z(c):
        for d in (1, 3, 2):
            x_copy(c, d).wait_recv()
        x_sum[c] = core_sum[c, :, x] + x_in[c, 0] + x_in[c, 1] + x_in[c, 2]
        for u in range(2):
            z_copy(c, u).start()

    def all_halves(*accs):
        def step(h, carry):
            c, w = h // 2, h % 2
            half_chunk(accs, c, w, stat_scr, bins_scr, turn_scr)

            @pl.when(h == 1)
            def _():
                pl.semaphore_wait(barrier, len(greeted))

            @pl.when(w == 1)
            def _():
                turn_chunk(c, turn_scr, hist)
                core_copy(c).start()

            @pl.when((w == 0) & (c >= 1))
            def _():
                start_x(c - 1)

            @pl.when((w == 0) & (c >= 2))
            def _():
                start_z(c - 2)

            return carry

        lax.fori_loop(0, 8, step, 0)

    pl.run_scoped(all_halves, *[pltpu.ACC(q % 2)((16, TILE), F32) for q in range(PAIRS)])

    add_core(3)
    for d in (2, 1, 3, 0):
        last_z_copy(d).start()
        if d:
            last_x_copy(d).start()
    start_z(2)
    block = core_sum[3, 1, x]
    for c in range(2):
        for u in range(2):
            z_copy(c, u).wait_recv()
            block = block + z_in[2 - c if u else 3 + c]
    for d in range(NX):
        last_z_copy(d).wait_recv()
        block = block + last_z[d]
        if d:
            last_x_copy(d).wait_recv()
            block = block + last_x[d - 1]
    for u in range(2):
        z_copy(2, u).wait_recv()
        block = block + z_in[0 if u else 5]

    top = finish(block, gain_ref)
    rounds = ([other], x_peer[1:], [at(0, d, core) for d in range(1, NZ)], y_peer[1:])
    top_copies = []
    for stage, peers in enumerate(rounds):
        top_out[stage] = top
        sent = []
        for k, peer in enumerate(peers):
            s = copy(top_out.at[stage], top_in.at[stage, k], top_send.at[stage, k], top_recv.at[stage, k], peer)
            s.start()
            sent.append(s)
        for k, s in enumerate(sent):
            s.wait_recv()
            top = jnp.maximum(top, top_in[stage, k])
        top_copies += sent
    for leaf in range(4):
        best_ref[leaf] = jnp.max(top[:, 32 * leaf : 32 * (leaf + 1)])
    for c in range(4):
        core_copy(c).wait_send()
    for c in range(3):
        for d in range(1, NX):
            x_copy(c, d).wait_send()
        for u in range(2):
            z_copy(c, u).wait_send()
    for d in range(NX):
        last_z_copy(d).wait_send()
        if d:
            last_x_copy(d).wait_send()
    for s in top_copies:
        s.wait_send()


def body(bin_values, leaf_ids, treated, gradient, hessian):
    shape = (ROWS // 128, 128)
    dma = pltpu.SemaphoreType.DMA
    block = (8, 512)
    gain, best = pl.pallas_call(
        kernel,
        out_shape=(jax.ShapeDtypeStruct((8, 128), F32), jax.ShapeDtypeStruct((4,), F32)),
        in_specs=[pl.BlockSpec(memory_space=pltpu.HBM)] * 5,
        out_specs=(pl.BlockSpec(memory_space=pltpu.VMEM), pl.BlockSpec(memory_space=pltpu.SMEM)),
        scratch_shapes=[
            pltpu.VMEM((ROWS, FEATS), jnp.int32),
            pltpu.VMEM(shape, jnp.int32),
            pltpu.VMEM(shape, jnp.int32),
            pltpu.VMEM(shape, BF),
            pltpu.VMEM(shape, BF),
            pltpu.VMEM((16, ROWS), BF),
            pltpu.VMEM((4, ROWS, 128), BF),
            pltpu.VMEM((512, 128), F32),
            pltpu.VMEM((4, 2, 2, NX) + block, F32),
            pltpu.VMEM((4, 2, NX) + block, F32),
            pltpu.VMEM((4, 2, NX) + block, F32),
            pltpu.VMEM((3, NX - 1, 2) + block, F32),
            pltpu.VMEM((3, 2) + block, F32),
            pltpu.VMEM((6,) + block, F32),
            pltpu.VMEM((NX - 1,) + block, F32),
            pltpu.VMEM((NX,) + block, F32),
            pltpu.VMEM((4, 1, 128), F32),
            pltpu.VMEM((4, 7, 1, 128), F32),
            dma((5,)), dma((4,)), dma((4,)), dma((3, 3)), dma((3, 3)), dma((6,)), dma((6,)),
            dma((3,)), dma((3,)), dma((4,)), dma((4,)), dma((4, 7)), dma((4, 7)),
        ],
        compiler_params=pltpu.CompilerParams(collective_id=0, has_side_effects=True, vmem_limit_bytes=56 << 20),
    )(bin_values, leaf_ids.reshape(shape), treated.reshape(shape), gradient.reshape(shape), hessian.reshape(shape))
    return gain.reshape(4, 2, 128), best


def solution(mesh):
    in_specs = (P("row", "feat"), P("row"), P("row"), P("row"), P("row"))
    out_specs = (P(None, ("feat", "row"), None), P())
    return jax.shard_map(body, mesh=mesh, in_specs=in_specs, out_specs=out_specs, check_vma=False)
```

time: 375 us -> 50.4 us (0.13)
  waiting for transfers between devices: 201 us -> 0 us
  blocking collectives: 97.1 us -> 0 us
  matrix products: 57.7 us -> 0 us
  Pallas kernels: 0 us -> 47.4 us
  between operations: 14.1 us -> 0.65 us
    psum x1 -> x0, waiting for transfers between devices: 201 us -> none  [body(): lax.psum(lax.map(one_block, blocks).reshape(feat_count, 4 * leaf_count, b...]
    pmax x1 -> x0, blocking collectives: 97.1 us -> none  [body(): best_gain = lax.pmax(jnp.max(gains_local, axis=(0, 2)), ('feat', 'row'))]
    dot_general x17 -> x0, matrix products: 57.7 us -> none  [the longest x16 56.8 us: one_block(): jnp.einsum('rc,rfb->fcb', stat_rows, one_hot, preferred_element_type=jnp....]
    pallas_call x0 -> x1, Pallas kernels: none -> 47.4 us  [body(): pl.pallas_call(kernel, out_shape=(jax.ShapeDtypeStruct((8, 128), F32), ja...]
  transfers between devices with their start and end apart: 1 -> 0, of which waited for: 1 -> 0; matrix products, arithmetic and copies ran while one was open for 0% -> 0% of each run, Pallas kernels for 0% -> 0%
where the time goes in v3:
time: 50.4 us; the launch traced here: 49.9 us
  Pallas kernels  47.4 us (94%)
  local copies, waits for them, and re-layouts  1.82 us (4%)
  between operations  0.65 us (1%)
    pallas_call x1, Pallas kernels, body(): pl.pallas_call(kernel, out_shape=(jax.ShapeDtypeStruct((8, 128), F32), ja...  47.4 us
    unnamed x6, local copies, waits for them, and re-layouts  1.82 us

profile of v3, /device:TPU:1, one launch (start us, length us, event | category | flops | bytes accessed | tf_op | source)
XLA Modules:
  0.0 49.9 jit_solution(4981950027584148512)
XLA Ops:
  0.6 47.4 %shard_map.68 = (f32[8,128]{1,0:T(8,128)}, f32[4]{0:T(128)}) custom-call(s32[2048,128]{1,0:T(8,128)} %bins_hbm.1, s32[16,128]{1,0:T(8,128)} %bitcast.5, s32[16,128]{1,0:T(8,128)} %bitcast.6, bf16[16,128]{1,0:T(8,128)(2,1)} %bitcast.7, bf16[16,128]{1,0:T(8,128)(2,1)} %bitcast.8), custom_call_target="tpu_custom_call" | custom-call | tf_op jit(solution)/shard_map/pallas_call | solution.py:297
  48.1 0.0 copy-start
  48.1 0.7 %copy-done = f32[8,128]{1,0:T(8,128)S(1)} copy-done((f32[8,128]{1,0:T(8,128)S(1)}, f32[8,128]{1,0:T(8,128)}, u32[]{:S(2)}) %copy-start) | copy-done | bytes 4120
  48.7 0.0 copy-start.1
  48.7 0.6 %copy.9 = f32[4,2,128]{2,1,0:T(2,128)} copy(f32[4,2,128]{2,1,0:T(2,128)S(1)} %bitcast.9) | data formatting | bytes 8192
  49.3 0.0 copy-done.1
  49.4 0.5 %copy.10 = f32[4]{0:T(128)} copy(f32[4]{0:T(128)S(1)} %copy-done.1) | data formatting | bytes 32
Async XLA Ops:
  48.1 0.7 %copy-start = (f32[8,128]{1,0:T(8,128)S(1)}, f32[8,128]{1,0:T(8,128)}, u32[]{:S(2)}) copy-start(f32[8,128]{1,0:T(8,128)} %get-tuple-element.4) | copy-start | bytes 12292
  48.7 0.6 %copy-start.1 = (f32[4]{0:T(128)S(1)}, f32[4]{0:T(128)}, u32[]{:S(2)}) copy-start(f32[4]{0:T(128)} %get-tuple-element.9) | copy-start | bytes 52

commit v4 on v3

--- a/solution.py
+++ b/solution.py
@@ -94,7 +94,7 @@
     return grad_t * value_t + grad_c * value_c + (hess_t + hess_c) * spread * spread
 
 
-def finish(block, gain_ref):
+def finish(block):
     x = jnp.concatenate([block[:, 128 * k : 128 * (k + 1)] for k in range(4)], axis=0)
     low = lax.broadcasted_iota(jnp.int32, (32, 128), 1) % 32
     sub = lax.broadcasted_iota(jnp.int32, (32, 128), 0) % 8
@@ -110,6 +110,10 @@
     parent = parent + jnp.where((sub >= 4) & (sub < 6), pltpu.roll(parent, 30, 0), 0.0)
     parent = parent + jnp.where(sub < 4, pltpu.roll(parent, 28, 0), 0.0)
     gain = score(left) + score(parent - left) - score(parent)
+    return gain
+
+
+def store_gain(gain, gain_ref):
     lane_block = lax.broadcasted_iota(jnp.int32, (8, 128), 1) // 32
     row_block = lax.broadcasted_iota(jnp.int32, (8, 128), 0) // 2
     out = gain
@@ -117,7 +121,6 @@
         moved = pltpu.roll(pltpu.roll(gain, 32 * d, 1), 8 - 2 * d, 0)
         out = jnp.where((lane_block + 4 - row_block) % 4 == d, moved, out)
     gain_ref[...] = out
-    return jnp.max(gain, axis=0, keepdims=True)
 
 
 def kernel(
@@ -259,7 +262,22 @@
         z_copy(2, u).wait_recv()
         block = block + z_in[0 if u else 5]
 
-    top = finish(block, gain_ref)
+    gain = finish(block)
+    top = jnp.max(gain, axis=0, keepdims=True)
+
+    def wait_sends():
+        for c in range(4):
+            core_copy(c).wait_send()
+        for c in range(3):
+            for d in range(1, NX):
+                x_copy(c, d).wait_send()
+            for u in range(2):
+                z_copy(c, u).wait_send()
+        for d in range(NX):
+            last_z_copy(d).wait_send()
+            if d:
+                last_x_copy(d).wait_send()
+
     rounds = ([other], x_peer[1:], [at(0, d, core) for d in range(1, NZ)], y_peer[1:])
     top_copies = []
     for stage, peers in enumerate(rounds):
@@ -269,23 +287,20 @@
             s = copy(top_out.at[stage], top_in.at[stage, k], top_send.at[stage, k], top_recv.at[stage, k], peer)
             s.start()
             sent.append(s)
+        if stage == 0:
+            store_gain(gain, gain_ref)
+        if stage == 2:
+            wait_sends()
+        if stage:
+            for s in top_copies:
+                s.wait_send()
+            top_copies = []
         for k, s in enumerate(sent):
             s.wait_recv()
             top = jnp.maximum(top, top_in[stage, k])
         top_copies += sent
     for leaf in range(4):
         best_ref[leaf] = jnp.max(top[:, 32 * leaf : 32 * (leaf + 1)])
-    for c in range(4):
-        core_copy(c).wait_send()
-    for c in range(3):
-        for d in range(1, NX):
-            x_copy(c, d).wait_send()
-        for u in range(2):
-            z_copy(c, u).wait_send()
-    for d in range(NX):
-        last_z_copy(d).wait_send()
-        if d:
-            last_x_copy(d).wait_send()
     for s in top_copies:
         s.wait_send()
 
@@ -294,6 +309,10 @@
     shape = (ROWS // 128, 128)
     dma = pltpu.SemaphoreType.DMA
     block = (8, 512)
+    bin_values, leaf_ids, treated, gradient, hessian = (
+        pltpu.with_memory_space_constraint(v, pltpu.HBM)
+        for v in (bin_values, leaf_ids.reshape(shape), treated.reshape(shape), gradient.reshape(shape), hessian.reshape(shape))
+    )
     gain, best = pl.pallas_call(
         kernel,
         out_shape=(jax.ShapeDtypeStruct((8, 128), F32), jax.ShapeDtypeStruct((4,), F32)),
@@ -321,8 +340,8 @@
             dma((5,)), dma((4,)), dma((4,)), dma((3, 3)), dma((3, 3)), dma((6,)), dma((6,)),
             dma((3,)), dma((3,)), dma((4,)), dma((4,)), dma((4, 7)), dma((4, 7)),
         ],
-        compiler_params=pltpu.CompilerParams(collective_id=0, has_side_effects=True, vmem_limit_bytes=56 << 20),
-    )(bin_values, leaf_ids.reshape(shape), treated.reshape(shape), gradient.reshape(shape), hessian.reshape(shape))
+        compiler_params=pltpu.CompilerParams(collective_id=0, has_side_effects=True, vmem_limit_bytes=24 << 20),
+    )(bin_values, leaf_ids, treated, gradient, hessian)
     return gain.reshape(4, 2, 128), best
 
 

time: 50.4 us -> 49.5 us (0.982)
  local copies, waits for them, and re-layouts: 1.82 us -> 1.11 us
    unnamed x6 -> x2, local copies, waits for them, and re-layouts: 1.82 us -> 1.11 us
where the time goes in v4:
time: 49.5 us; the launch traced here: 49 us
  Pallas kernels  47.3 us (96%)
  local copies, waits for them, and re-layouts  1.11 us (2%)
  between operations  0.64 us (1%)
    pallas_call x1, Pallas kernels, body(): pl.pallas_call(kernel, out_shape=(jax.ShapeDtypeStruct((8, 128), F32), ja...  47.3 us
    unnamed x2, local copies, waits for them, and re-layouts  1.11 us

profile of v4, /device:TPU:1, one launch (start us, length us, event | category | flops | bytes accessed | tf_op | source)
XLA Modules:
  0.0 49.0 jit_solution(1802033237194563021)
XLA Ops:
  0.6 47.3 %shard_map.68 = (f32[8,128]{1,0:T(8,128)S(1)}, f32[4]{0:T(128)S(1)}) custom-call(s32[2048,128]{1,0:T(8,128)} %bins_hbm.1, s32[16,128]{1,0:T(8,128)} %bitcast.6, s32[16,128]{1,0:T(8,128)} %bitcast.7, bf16[16,128]{1,0:T(8,128)(2,1)} %bitcast.8, bf16[16,128]{1,0:T(8,128)(2,1)} %bitcast.9), custom_call_target="tpu_custom_call" | custom-call | tf_op jit(solution)/shard_map/pallas_call | solution.py:316
  47.9 0.6 %copy.9 = f32[4,2,128]{2,1,0:T(2,128)} copy(f32[4,2,128]{2,1,0:T(2,128)S(1)} %bitcast.5) | data formatting | bytes 8192
  48.5 0.5 %copy.10 = f32[4]{0:T(128)} copy(f32[4]{0:T(128)S(1)} %get-tuple-element.9) | data formatting | bytes 32

commit v5 on v4

--- a/solution.py
+++ b/solution.py
@@ -64,13 +64,13 @@
     one, zero = jnp.ones(shape, BF), jnp.zeros(shape, BF)
     group = lax.broadcasted_iota(jnp.int32, (16, 128), 1) % 8 // 2
     first = 2 * PAIRS * w
-    wanted = [(group * 32 + (first + q)).astype(F32).astype(BF)[None] for q in range(2 * PAIRS)]
+    past = [(group * 32 + (first + q + 1)).astype(F32).astype(BF)[None] for q in range(2 * PAIRS)]
     for k in range(TILES):
         rows = slice(k * TILE, (k + 1) * TILE)
         bins = bins_scr[c, rows, :].reshape(shape)
         stat = stat_scr[:, rows]
         for q in range(PAIRS):
-            hot = [jnp.where(bins == wanted[2 * q + e], one, zero).reshape(TILE, 128) for e in range(2)]
+            hot = [jnp.clip(past[2 * q + e] - bins, zero, one).reshape(TILE, 128) for e in range(2)]
             reg = (k * (PAIRS // 2) + q // 2) % 2
             pltpu.matmul_push_rhs(jnp.concatenate(hot, axis=1), staging_register=reg, mxu_index=q % 2)
             pltpu.matmul_acc_lhs(accs[q], stat, load_staged_rhs=reg)
@@ -95,20 +95,15 @@
 
 
 def finish(block):
-    x = jnp.concatenate([block[:, 128 * k : 128 * (k + 1)] for k in range(4)], axis=0)
-    low = lax.broadcasted_iota(jnp.int32, (32, 128), 1) % 32
+    left = jnp.concatenate([block[:, 128 * k : 128 * (k + 1)] for k in range(4)], axis=0)
+    leaf = lax.broadcasted_iota(jnp.int32, (32, 128), 1) // 32
     sub = lax.broadcasted_iota(jnp.int32, (32, 128), 0) % 8
-    for shift in (1, 2, 4, 8, 16):
-        x = x + jnp.where(low >= shift, pltpu.roll(x, shift, 1), 0.0)
-    total = jnp.where(low == 31, x, 0.0)
-    for shift in (1, 2, 4, 8, 16):
-        total = total + jnp.where(low <= 31 - shift, pltpu.roll(total, 128 - shift, 1), 0.0)
-    upto = total + jnp.where(sub >= 2, pltpu.roll(total, 2, 0), 0.0)
-    upto = upto + jnp.where(sub >= 4, pltpu.roll(upto, 4, 0), 0.0)
-    left = x + jnp.where(sub >= 2, pltpu.roll(upto, 2, 0), 0.0)
-    parent = jnp.where(sub >= 6, upto, 0.0)
-    parent = parent + jnp.where((sub >= 4) & (sub < 6), pltpu.roll(parent, 30, 0), 0.0)
-    parent = parent + jnp.where(sub < 4, pltpu.roll(parent, 28, 0), 0.0)
+    last = jnp.where(sub >= 6, left, 0.0)
+    last = last + jnp.where((sub >= 4) & (sub < 6), pltpu.roll(last, 30, 0), 0.0)
+    last = last + jnp.where(sub < 4, pltpu.roll(last, 28, 0), 0.0)
+    parent = jnp.broadcast_to(last[:, 127:128], (32, 128))
+    for k in range(3):
+        parent = jnp.where(leaf == k, jnp.broadcast_to(last[:, 32 * k + 31 : 32 * k + 32], (32, 128)), parent)
     gain = score(left) + score(parent - left) - score(parent)
     return gain
 

time: 49.5 us -> 46.7 us (0.943)
  Pallas kernels: 47.3 us -> 44.8 us
    pallas_call x1, Pallas kernels: 47.3 us -> 44.8 us  [body(): pl.pallas_call(kernel, out_shape=(jax.ShapeDtypeStruct((8, 128), F32), ja...]
where the time goes in v5:
time: 46.7 us; the launch traced here: 46.5 us
  Pallas kernels  44.8 us (96%)
  local copies, waits for them, and re-layouts  1.11 us (2%)
  between operations  0.64 us (1%)
    pallas_call x1, Pallas kernels, body(): pl.pallas_call(kernel, out_shape=(jax.ShapeDtypeStruct((8, 128), F32), ja...  44.8 us
    unnamed x2, local copies, waits for them, and re-layouts  1.11 us

profile of v5, /device:TPU:1, one launch (start us, length us, event | category | flops | bytes accessed | tf_op | source)
XLA Modules:
  0.0 46.5 jit_solution(5886891671653700006)
XLA Ops:
  0.6 44.8 %shard_map.68 = (f32[8,128]{1,0:T(8,128)S(1)}, f32[4]{0:T(128)S(1)}) custom-call(s32[2048,128]{1,0:T(8,128)} %bins_hbm.1, s32[16,128]{1,0:T(8,128)} %bitcast.6, s32[16,128]{1,0:T(8,128)} %bitcast.7, bf16[16,128]{1,0:T(8,128)(2,1)} %bitcast.8, bf16[16,128]{1,0:T(8,128)(2,1)} %bitcast.9), custom_call_target="tpu_custom_call" | custom-call | tf_op jit(solution)/shard_map/pallas_call | solution.py:311
  45.4 0.6 %copy.9 = f32[4,2,128]{2,1,0:T(2,128)} copy(f32[4,2,128]{2,1,0:T(2,128)S(1)} %bitcast.5) | data formatting | bytes 8192
  46.0 0.5 %copy.10 = f32[4]{0:T(128)} copy(f32[4]{0:T(128)S(1)} %get-tuple-element.9) | data formatting | bytes 32

commit v6 on v5

--- a/solution.py
+++ b/solution.py
@@ -39,7 +39,7 @@
     return [jnp.concatenate(orders[:2], axis=1), jnp.concatenate(orders[2:], axis=1)]
 
 
-def spread_bins(accs, orders, bins_ref, bins_scr):
+def spread_bins(accs, orders, loads, bins_ref, bins_scr):
     def drain(r):
         rows = slice(r * TILE, (r + 1) * TILE)
         for p in range(2):
@@ -50,6 +50,8 @@
     for p in range(2):
         pltpu.matmul_push_rhs(orders[p], staging_register=0, mxu_index=p)
     for r in range(TILES):
+        if r % 2 == 0:
+            loads[r // 2].wait()
         block = bins_ref[r * TILE : (r + 1) * TILE, :].astype(F32).astype(BF)
         block = jnp.concatenate([block, block], axis=1)
         for p in range(2):
@@ -138,15 +140,9 @@
     x_peer = [at(d, 0, core) for d in range(NX)]
     y_peer = [(lax.rem(feat + d, NY), row) for d in range(NY)]
 
-    loads = [
-        pltpu.make_async_copy(src, dst, load_sem.at[k])
-        for k, (src, dst) in enumerate(
-            zip(
-                (leaf_hbm, arm_hbm, grad_hbm, hess_hbm, bins_hbm),
-                (leaf_ref, arm_ref, grad_ref, hess_ref, bins_ref),
-            )
-        )
-    ]
+    pairs = [(leaf_hbm, leaf_ref), (arm_hbm, arm_ref), (grad_hbm, grad_ref), (hess_hbm, hess_ref)]
+    pairs += [(bins_hbm.at[pl.ds(k * 512, 512)], bins_ref.at[pl.ds(k * 512, 512)]) for k in range(4)]
+    loads = [pltpu.make_async_copy(src, dst, load_sem.at[k]) for k, (src, dst) in enumerate(pairs)]
     for load in loads:
         load.start()
     barrier = pltpu.get_barrier_semaphore()
@@ -159,9 +155,8 @@
         load.wait()
     load_stats(leaf_ref, arm_ref, grad_ref, hess_ref, stat_scr)
     orders = lane_orders(z)
-    loads[4].wait()
     pl.run_scoped(
-        lambda *accs: spread_bins(accs, orders, bins_ref, bins_scr),
+        lambda *accs: spread_bins(accs, orders, loads[4:], bins_ref, bins_scr),
         *[pltpu.ACC(q % 2)((TILE, TILE), F32) for q in range(4)],
     )
 
@@ -172,6 +167,10 @@
 
     def core_copy(c):
         return copy(hist.at[c, 1 - core], core_in.at[c], core_send.at[c], core_recv.at[c], other)
+
+    def last_core_copy(u):
+        k = 3 + u
+        return copy(hist.at[3, 1 - core, u], core_in.at[3, u], core_send.at[k], core_recv.at[k], other)
 
     def x_copy(c, d):
         return copy(
@@ -220,8 +219,16 @@
             @pl.when(w == 1)
             def _():
                 turn_chunk(c, turn_scr, hist)
+
+            @pl.when((w == 1) & (c < 3))
+            def _():
                 core_copy(c).start()
 
+            @pl.when((w == 1) & (c == 3))
+            def _():
+                for u in range(2):
+                    last_core_copy(u).start()
+
             @pl.when((w == 0) & (c >= 1))
             def _():
                 start_x(c - 1)
@@ -236,11 +243,14 @@
 
     pl.run_scoped(all_halves, *[pltpu.ACC(q % 2)((16, TILE), F32) for q in range(PAIRS)])
 
-    add_core(3)
-    for d in (2, 1, 3, 0):
-        last_z_copy(d).start()
-        if d:
-            last_x_copy(d).start()
+    for u in range(2):
+        last_core_copy(u).wait_recv()
+        core_sum[3, u] = hist[3, core, u] + core_in[3, u]
+        for d in (2, 1, 3, 0):
+            if u == 0:
+                last_z_copy(d).start()
+            elif d:
+                last_x_copy(d).start()
     start_z(2)
     block = core_sum[3, 1, x]
     for c in range(2):
@@ -261,9 +271,10 @@
     top = jnp.max(gain, axis=0, keepdims=True)
 
     def wait_sends():
-        for c in range(4):
+        for u in range(2):
+            last_core_copy(u).wait_send()
+        for c in range(3):
             core_copy(c).wait_send()
-        for c in range(3):
             for d in range(1, NX):
                 x_copy(c, d).wait_send()
             for u in range(2):
@@ -273,7 +284,13 @@
             if d:
                 last_x_copy(d).wait_send()
 
-    rounds = ([other], x_peer[1:], [at(0, d, core) for d in range(1, NZ)], y_peer[1:])
+    near_last = (4, 3, 5, 2, 6, 1, 7)
+    rounds = (
+        [other],
+        [x_peer[d] for d in (2, 1, 3)],
+        [at(0, d, core) for d in near_last],
+        [y_peer[d] for d in near_last],
+    )
     top_copies = []
     for stage, peers in enumerate(rounds):
         top_out[stage] = top
@@ -290,14 +307,22 @@
             for s in top_copies:
                 s.wait_send()
             top_copies = []
-        for k, s in enumerate(sent):
+        for s in reversed(sent):
             s.wait_recv()
+        for k in range(len(sent)):
             top = jnp.maximum(top, top_in[stage, k])
         top_copies += sent
-    for leaf in range(4):
-        best_ref[leaf] = jnp.max(top[:, 32 * leaf : 32 * (leaf + 1)])
+    best_ref[...] = top
     for s in top_copies:
         s.wait_send()
+
+
+def write_kernel(gain_ref, top_ref, gain_hbm, best_ref, sem):
+    write = pltpu.make_async_copy(gain_ref, gain_hbm, sem)
+    write.start()
+    for leaf in range(4):
+        best_ref[leaf] = jnp.max(top_ref[:, 32 * leaf : 32 * (leaf + 1)])
+    write.wait()
 
 
 def body(bin_values, leaf_ids, treated, gradient, hessian):
@@ -308,11 +333,11 @@
         pltpu.with_memory_space_constraint(v, pltpu.HBM)
         for v in (bin_values, leaf_ids.reshape(shape), treated.reshape(shape), gradient.reshape(shape), hessian.reshape(shape))
     )
-    gain, best = pl.pallas_call(
+    gain, top = pl.pallas_call(
         kernel,
-        out_shape=(jax.ShapeDtypeStruct((8, 128), F32), jax.ShapeDtypeStruct((4,), F32)),
+        out_shape=(jax.ShapeDtypeStruct((8, 128), F32), jax.ShapeDtypeStruct((1, 128), F32)),
         in_specs=[pl.BlockSpec(memory_space=pltpu.HBM)] * 5,
-        out_specs=(pl.BlockSpec(memory_space=pltpu.VMEM), pl.BlockSpec(memory_space=pltpu.SMEM)),
+        out_specs=(pl.BlockSpec(memory_space=pltpu.VMEM),) * 2,
         scratch_shapes=[
             pltpu.VMEM((ROWS, FEATS), jnp.int32),
             pltpu.VMEM(shape, jnp.int32),
@@ -332,11 +357,20 @@
             pltpu.VMEM((NX,) + block, F32),
             pltpu.VMEM((4, 1, 128), F32),
             pltpu.VMEM((4, 7, 1, 128), F32),
-            dma((5,)), dma((4,)), dma((4,)), dma((3, 3)), dma((3, 3)), dma((6,)), dma((6,)),
+            dma((8,)), dma((5,)), dma((5,)), dma((3, 3)), dma((3, 3)), dma((6,)), dma((6,)),
             dma((3,)), dma((3,)), dma((4,)), dma((4,)), dma((4, 7)), dma((4, 7)),
         ],
         compiler_params=pltpu.CompilerParams(collective_id=0, has_side_effects=True, vmem_limit_bytes=24 << 20),
     )(bin_values, leaf_ids, treated, gradient, hessian)
+    vmem = pl.BlockSpec(memory_space=pltpu.VMEM)
+    gain, best = pl.pallas_call(
+        write_kernel,
+        out_shape=(jax.ShapeDtypeStruct((8, 128), F32), jax.ShapeDtypeStruct((4,), F32)),
+        in_specs=[vmem, vmem],
+        out_specs=(pl.BlockSpec(memory_space=pltpu.HBM), pl.BlockSpec(memory_space=pltpu.SMEM)),
+        scratch_shapes=[dma(())],
+        compiler_params=pltpu.CompilerParams(vmem_limit_bytes=1 << 20),
+    )(gain, top)
     return gain.reshape(4, 2, 128), best
 
 

time: 46.7 us -> 46 us (0.985)
  local copies, waits for them, and re-layouts: 1.11 us -> 0 us
  Pallas kernels: 44.8 us -> 45.3 us
    pallas_call x0 -> x1, Pallas kernels: none -> 1.12 us  [body(): pl.pallas_call(write_kernel, out_shape=(jax.ShapeDtypeStruct((8, 128), F3...]
    unnamed x2 -> x0, local copies, waits for them, and re-layouts: 1.11 us -> none
    pallas_call x1, Pallas kernels: 44.8 us -> 44.1 us  [body(): pl.pallas_call(kernel, out_shape=(jax.ShapeDtypeStruct((8, 128), F32), ja...]
where the time goes in v6:
time: 46 us; the launch traced here: 45.9 us
  Pallas kernels  45.3 us (98%)
  between operations  0.64 us (1%)
    pallas_call x1, Pallas kernels, body(): pl.pallas_call(kernel, out_shape=(jax.ShapeDtypeStruct((8, 128), F32), ja...  44.1 us
    pallas_call x1, Pallas kernels, body(): pl.pallas_call(write_kernel, out_shape=(jax.ShapeDtypeStruct((8, 128), F3...  1.12 us

profile of v6, /device:TPU:1, one launch (start us, length us, event | category | flops | bytes accessed | tf_op | source)
XLA Modules:
  0.0 45.9 jit_solution(15731953565316238516)
XLA Ops:
  0.6 44.1 %shard_map.68 = (f32[8,128]{1,0:T(8,128)S(1)}, f32[1,128]{1,0:T(1,128)S(1)}) custom-call(s32[2048,128]{1,0:T(8,128)} %bins_hbm.1, s32[16,128]{1,0:T(8,128)} %bitcast.5, s32[16,128]{1,0:T(8,128)} %bitcast.6, bf16[16,128]{1,0:T(8,128)(2,1)} %bitcast.7, bf16[16,128]{1,0:T(8,128)(2,1)} %bitcast.8), custom_call_target="tpu_custom_call" | custom-call | tf_op jit(solution)/shard_map/pallas_call | solution.py:336
  44.8 1.1 %shard_map.69 = (f32[8,128]{1,0:T(8,128)}, f32[4]{0:T(128)}) custom-call(f32[8,128]{1,0:T(8,128)S(1)} %get-tuple-element.6.gain_ref, f32[1,128]{1,0:T(1,128)S(1)} %get-tuple-element.7.top_ref), custom_call_target="tpu_custom_call" | custom-call | tf_op jit(solution)/shard_map/pallas_call | solution.py:366

commit v7 on v6

--- a/solution.py
+++ b/solution.py
@@ -8,6 +8,7 @@
 MESH = pl.DeviceIdType.MESH
 BF = jnp.bfloat16
 F32 = jnp.float32
+F8 = jnp.float8_e4m3fn
 ROWS = 2048
 FEATS = 128
 TILE = 256
@@ -43,7 +44,7 @@
     def drain(r):
         rows = slice(r * TILE, (r + 1) * TILE)
         for p in range(2):
-            spread = pltpu.matmul_pop(accs[2 * (r % 2) + p]).astype(BF)
+            spread = pltpu.matmul_pop(accs[2 * (r % 2) + p]).astype(jnp.int32).astype(jnp.int8)
             bins_scr[2 * p, rows, :] = spread[:, :128]
             bins_scr[2 * p + 1, rows, :] = spread[:, 128:]
 
@@ -62,17 +63,17 @@
 
 
 def half_chunk(accs, c, w, stat_scr, bins_scr, turn_scr):
-    shape = (16, 16, 128)
-    one, zero = jnp.ones(shape, BF), jnp.zeros(shape, BF)
-    group = lax.broadcasted_iota(jnp.int32, (16, 128), 1) % 8 // 2
+    shape = (TILE // 32, 32, 128)
+    one, zero = jnp.ones(shape, F8), jnp.zeros(shape, F8)
+    group = lax.broadcasted_iota(jnp.int32, (32, 128), 1) % 8 // 2
     first = 2 * PAIRS * w
-    past = [(group * 32 + (first + q + 1)).astype(F32).astype(BF)[None] for q in range(2 * PAIRS)]
+    last = [(group * 32 + (first + q)).astype(jnp.int8)[None] for q in range(2 * PAIRS)]
     for k in range(TILES):
         rows = slice(k * TILE, (k + 1) * TILE)
         bins = bins_scr[c, rows, :].reshape(shape)
         stat = stat_scr[:, rows]
         for q in range(PAIRS):
-            hot = [jnp.clip(past[2 * q + e] - bins, zero, one).reshape(TILE, 128) for e in range(2)]
+            hot = [jnp.where(bins <= last[2 * q + e], one, zero).reshape(TILE, 128) for e in range(2)]
             reg = (k * (PAIRS // 2) + q // 2) % 2
             pltpu.matmul_push_rhs(jnp.concatenate(hot, axis=1), staging_register=reg, mxu_index=q % 2)
             pltpu.matmul_acc_lhs(accs[q], stat, load_staged_rhs=reg)
@@ -345,7 +346,7 @@
             pltpu.VMEM(shape, BF),
             pltpu.VMEM(shape, BF),
             pltpu.VMEM((16, ROWS), BF),
-            pltpu.VMEM((4, ROWS, 128), BF),
+            pltpu.VMEM((4, ROWS, 128), jnp.int8),
             pltpu.VMEM((512, 128), F32),
             pltpu.VMEM((4, 2, 2, NX) + block, F32),
             pltpu.VMEM((4, 2, NX) + block, F32),

time: 46 us -> 45 us (0.978)
  Pallas kernels: 45.3 us -> 44.2 us
    pallas_call x1, Pallas kernels: 44.1 us -> 43.1 us  [body(): pl.pallas_call(kernel, out_shape=(jax.ShapeDtypeStruct((8, 128), F32), ja...]
where the time goes in v7:
time: 45 us; the launch traced here: 44.9 us
  Pallas kernels  44.2 us (98%)
  between operations  0.64 us (1%)
    pallas_call x1, Pallas kernels, body(): pl.pallas_call(kernel, out_shape=(jax.ShapeDtypeStruct((8, 128), F32), ja...  43.1 us
    pallas_call x1, Pallas kernels, body(): pl.pallas_call(write_kernel, out_shape=(jax.ShapeDtypeStruct((8, 128), F3...  1.12 us

profile of v7, /device:TPU:1, one launch (start us, length us, event | category | flops | bytes accessed | tf_op | source)
XLA Modules:
  0.0 44.9 jit_solution(7699151206760990876)
XLA Ops:
  0.6 43.1 %shard_map.68 = (f32[8,128]{1,0:T(8,128)S(1)}, f32[1,128]{1,0:T(1,128)S(1)}) custom-call(s32[2048,128]{1,0:T(8,128)} %bins_hbm.1, s32[16,128]{1,0:T(8,128)} %bitcast.5, s32[16,128]{1,0:T(8,128)} %bitcast.6, bf16[16,128]{1,0:T(8,128)(2,1)} %bitcast.7, bf16[16,128]{1,0:T(8,128)(2,1)} %bitcast.8), custom_call_target="tpu_custom_call" | custom-call | tf_op jit(solution)/shard_map/pallas_call | solution.py:337
  43.8 1.1 %shard_map.69 = (f32[8,128]{1,0:T(8,128)}, f32[4]{0:T(128)}) custom-call(f32[8,128]{1,0:T(8,128)S(1)} %get-tuple-element.6.gain_ref, f32[1,128]{1,0:T(1,128)S(1)} %get-tuple-element.7.top_ref), custom_call_target="tpu_custom_call" | custom-call | tf_op jit(solution)/shard_map/pallas_call | solution.py:367

commit v8 on v7

--- a/solution.py
+++ b/solution.py
@@ -230,13 +230,9 @@
                 for u in range(2):
                     last_core_copy(u).start()
 
-            @pl.when((w == 0) & (c >= 1))
+            @pl.when(((w == 1) & (c >= 1) & (c < 3)) | (h == 6))
             def _():
                 start_x(c - 1)
-
-            @pl.when((w == 0) & (c >= 2))
-            def _():
-                start_z(c - 2)
 
             return carry
 
@@ -252,7 +248,8 @@
                 last_z_copy(d).start()
             elif d:
                 last_x_copy(d).start()
-    start_z(2)
+    for c in range(3):
+        start_z(c)
     block = core_sum[3, 1, x]
     for c in range(2):
         for u in range(2):

time: 45 us -> 42.6 us (0.947)
  Pallas kernels: 44.2 us -> 41.9 us
    pallas_call x1, Pallas kernels: 43.1 us -> 40.7 us  [body(): pl.pallas_call(kernel, out_shape=(jax.ShapeDtypeStruct((8, 128), F32), ja...]
where the time goes in v8:
time: 42.6 us; the launch traced here: 42.5 us
  Pallas kernels  41.9 us (98%)
  between operations  0.64 us (2%)
    pallas_call x1, Pallas kernels, body(): pl.pallas_call(kernel, out_shape=(jax.ShapeDtypeStruct((8, 128), F32), ja...  40.7 us
    pallas_call x1, Pallas kernels, body(): pl.pallas_call(write_kernel, out_shape=(jax.ShapeDtypeStruct((8, 128), F3...  1.12 us

profile of v8, /device:TPU:1, one launch (start us, length us, event | category | flops | bytes accessed | tf_op | source)
XLA Modules:
  0.0 42.5 jit_solution(15007339398105581155)
XLA Ops:
  0.6 40.7 %shard_map.68 = (f32[8,128]{1,0:T(8,128)S(1)}, f32[1,128]{1,0:T(1,128)S(1)}) custom-call(s32[2048,128]{1,0:T(8,128)} %bins_hbm.1, s32[16,128]{1,0:T(8,128)} %bitcast.5, s32[16,128]{1,0:T(8,128)} %bitcast.6, bf16[16,128]{1,0:T(8,128)(2,1)} %bitcast.7, bf16[16,128]{1,0:T(8,128)(2,1)} %bitcast.8), custom_call_target="tpu_custom_call" | custom-call | tf_op jit(solution)/shard_map/pallas_call | solution.py:334
  41.4 1.1 %shard_map.69 = (f32[8,128]{1,0:T(8,128)}, f32[4]{0:T(128)}) custom-call(f32[8,128]{1,0:T(8,128)S(1)} %get-tuple-element.6.gain_ref, f32[1,128]{1,0:T(1,128)S(1)} %get-tuple-element.7.top_ref), custom_call_target="tpu_custom_call" | custom-call | tf_op jit(solution)/shard_map/pallas_call | solution.py:364

commit v9 on v8

--- a/solution.py
+++ b/solution.py
@@ -147,8 +147,9 @@
     for load in loads:
         load.start()
     barrier = pltpu.get_barrier_semaphore()
-    greeted = [other] + x_peer[1:] + [at(0, d, core) for d in range(1, NZ)] + y_peer[1:]
-    greeted += [at(d, e, core) for d in range(1, NX) for e in (1, NZ - 1)]
+    far = (4, 3, 5, 2, 6, 1, 7)
+    greeted = [at(0, d, core) for d in far] + [y_peer[d] for d in far]
+    greeted += [at(d, e, core) for d in (2, 1, 3) for e in (1, NZ - 1, 0)] + [other]
     for peer in greeted:
         pl.semaphore_signal(barrier, inc=1, device_id=peer, device_id_type=MESH)
 
@@ -213,26 +214,27 @@
             c, w = h // 2, h % 2
             half_chunk(accs, c, w, stat_scr, bins_scr, turn_scr)
 
-            @pl.when(h == 1)
+            @pl.when(w == 1)
+            def _():
+                turn_chunk(c, turn_scr, hist)
+
+            @pl.when(h == 2)
             def _():
                 pl.semaphore_wait(barrier, len(greeted))
-
-            @pl.when(w == 1)
-            def _():
-                turn_chunk(c, turn_scr, hist)
-
-            @pl.when((w == 1) & (c < 3))
+                core_copy(0).start()
+
+            @pl.when((h == 3) | (h == 5))
             def _():
                 core_copy(c).start()
 
-            @pl.when((w == 1) & (c == 3))
+            @pl.when(h == 7)
             def _():
                 for u in range(2):
                     last_core_copy(u).start()
 
-            @pl.when(((w == 1) & (c >= 1) & (c < 3)) | (h == 6))
-            def _():
-                start_x(c - 1)
+            @pl.when((h == 4) | (h == 5) | (h == 6))
+            def _():
+                start_x(h - 4)
 
             return carry
 
@@ -282,12 +284,11 @@
             if d:
                 last_x_copy(d).wait_send()
 
-    near_last = (4, 3, 5, 2, 6, 1, 7)
     rounds = (
         [other],
         [x_peer[d] for d in (2, 1, 3)],
-        [at(0, d, core) for d in near_last],
-        [y_peer[d] for d in near_last],
+        [at(0, d, core) for d in far],
+        [y_peer[d] for d in far],
     )
     top_copies = []
     for stage, peers in enumerate(rounds):

time: 42.6 us -> 43 us (level)
  no operation moved by 1% of the time
where the time goes in v9:
time: 43 us; the launch traced here: 42.9 us
  Pallas kernels  42.2 us (98%)
  between operations  0.64 us (1%)
    pallas_call x1, Pallas kernels, body(): pl.pallas_call(kernel, out_shape=(jax.ShapeDtypeStruct((8, 128), F32), ja...  41.1 us
    pallas_call x1, Pallas kernels, body(): pl.pallas_call(write_kernel, out_shape=(jax.ShapeDtypeStruct((8, 128), F3...  1.12 us

profile of v9, /device:TPU:1, one launch (start us, length us, event | category | flops | bytes accessed | tf_op | source)
XLA Modules:
  0.0 42.9 jit_solution(1748965350096750758)
XLA Ops:
  0.6 41.1 %shard_map.68 = (f32[8,128]{1,0:T(8,128)S(1)}, f32[1,128]{1,0:T(1,128)S(1)}) custom-call(s32[2048,128]{1,0:T(8,128)} %bins_hbm.1, s32[16,128]{1,0:T(8,128)} %bitcast.5, s32[16,128]{1,0:T(8,128)} %bitcast.6, bf16[16,128]{1,0:T(8,128)(2,1)} %bitcast.7, bf16[16,128]{1,0:T(8,128)(2,1)} %bitcast.8), custom_call_target="tpu_custom_call" | custom-call | tf_op jit(solution)/shard_map/pallas_call | solution.py:335
  41.7 1.1 %shard_map.69 = (f32[8,128]{1,0:T(8,128)}, f32[4]{0:T(128)}) custom-call(f32[8,128]{1,0:T(8,128)S(1)} %get-tuple-element.6.gain_ref, f32[1,128]{1,0:T(1,128)S(1)} %get-tuple-element.7.top_ref), custom_call_target="tpu_custom_call" | custom-call | tf_op jit(solution)/shard_map/pallas_call | solution.py:365

commit v10 on v8

--- a/solution.py
+++ b/solution.py
@@ -147,8 +147,9 @@
     for load in loads:
         load.start()
     barrier = pltpu.get_barrier_semaphore()
-    greeted = [other] + x_peer[1:] + [at(0, d, core) for d in range(1, NZ)] + y_peer[1:]
-    greeted += [at(d, e, core) for d in range(1, NX) for e in (1, NZ - 1)]
+    far = (4, 3, 5, 2, 6, 1, 7)
+    greeted = [at(0, d, core) for d in far] + [y_peer[d] for d in far]
+    greeted += [at(d, e, core) for d in (2, 1, 3) for e in (1, NZ - 1, 0)] + [other]
     for peer in greeted:
         pl.semaphore_signal(barrier, inc=1, device_id=peer, device_id_type=MESH)
 
@@ -240,6 +241,7 @@
 
     pl.run_scoped(all_halves, *[pltpu.ACC(q % 2)((16, TILE), F32) for q in range(PAIRS)])
 
+    start_z(0)
     for u in range(2):
         last_core_copy(u).wait_recv()
         core_sum[3, u] = hist[3, core, u] + core_in[3, u]
@@ -248,7 +250,7 @@
                 last_z_copy(d).start()
             elif d:
                 last_x_copy(d).start()
-    for c in range(3):
+    for c in range(1, 3):
         start_z(c)
     block = core_sum[3, 1, x]
     for c in range(2):
@@ -282,12 +284,11 @@
             if d:
                 last_x_copy(d).wait_send()
 
-    near_last = (4, 3, 5, 2, 6, 1, 7)
     rounds = (
         [other],
         [x_peer[d] for d in (2, 1, 3)],
-        [at(0, d, core) for d in near_last],
-        [y_peer[d] for d in near_last],
+        [at(0, d, core) for d in far],
+        [y_peer[d] for d in far],
     )
     top_copies = []
     for stage, peers in enumerate(rounds):

time: 42.6 us -> 42.4 us (level)
  no operation moved by 1% of the time
where the time goes in v10:
time: 42.4 us; the launch traced here: 42.3 us
  Pallas kernels  41.7 us (98%)
  between operations  0.64 us (2%)
    pallas_call x1, Pallas kernels, body(): pl.pallas_call(kernel, out_shape=(jax.ShapeDtypeStruct((8, 128), F32), ja...  40.5 us
    pallas_call x1, Pallas kernels, body(): pl.pallas_call(write_kernel, out_shape=(jax.ShapeDtypeStruct((8, 128), F3...  1.12 us

profile of v10, /device:TPU:1, one launch (start us, length us, event | category | flops | bytes accessed | tf_op | source)
XLA Modules:
  0.0 42.3 jit_solution(3295878211935582956)
XLA Ops:
  0.6 40.5 %shard_map.68 = (f32[8,128]{1,0:T(8,128)S(1)}, f32[1,128]{1,0:T(1,128)S(1)}) custom-call(s32[2048,128]{1,0:T(8,128)} %bins_hbm.1, s32[16,128]{1,0:T(8,128)} %bitcast.5, s32[16,128]{1,0:T(8,128)} %bitcast.6, bf16[16,128]{1,0:T(8,128)(2,1)} %bitcast.7, bf16[16,128]{1,0:T(8,128)(2,1)} %bitcast.8), custom_call_target="tpu_custom_call" | custom-call | tf_op jit(solution)/shard_map/pallas_call | solution.py:335
  41.2 1.1 %shard_map.69 = (f32[8,128]{1,0:T(8,128)}, f32[4]{0:T(128)}) custom-call(f32[8,128]{1,0:T(8,128)S(1)} %get-tuple-element.6.gain_ref, f32[1,128]{1,0:T(1,128)S(1)} %get-tuple-element.7.top_ref), custom_call_target="tpu_custom_call" | custom-call | tf_op jit(solution)/shard_map/pallas_call | solution.py:365

commit v11 on v10

--- a/solution.py
+++ b/solution.py
@@ -13,7 +13,7 @@
 FEATS = 128
 TILE = 256
 TILES = ROWS // TILE
-PAIRS = 8
+PAIRS = 16
 NX, NZ, NY = 4, 8, 8
 
 
@@ -62,12 +62,11 @@
     drain(TILES - 1)
 
 
-def half_chunk(accs, c, w, stat_scr, bins_scr, turn_scr):
+def sum_chunk(accs, c, stat_scr, bins_scr, turn_scr):
     shape = (TILE // 32, 32, 128)
     one, zero = jnp.ones(shape, F8), jnp.zeros(shape, F8)
     group = lax.broadcasted_iota(jnp.int32, (32, 128), 1) % 8 // 2
-    first = 2 * PAIRS * w
-    last = [(group * 32 + (first + q)).astype(jnp.int8)[None] for q in range(2 * PAIRS)]
+    last = [(group * 32 + q).astype(jnp.int8)[None] for q in range(2 * PAIRS)]
     for k in range(TILES):
         rows = slice(k * TILE, (k + 1) * TILE)
         bins = bins_scr[c, rows, :].reshape(shape)
@@ -80,7 +79,7 @@
     for q in range(PAIRS):
         sums = pltpu.matmul_pop(accs[q])
         for e in range(2):
-            turn_scr[pl.ds(first + 2 * q + e, 16, stride=32), :] = sums[:, e * 128 : (e + 1) * 128]
+            turn_scr[pl.ds(2 * q + e, 16, stride=32), :] = sums[:, e * 128 : (e + 1) * 128]
 
 
 def turn_chunk(c, turn_scr, hist):
@@ -209,37 +208,34 @@
         for u in range(2):
             z_copy(c, u).start()
 
-    def all_halves(*accs):
-        def step(h, carry):
-            c, w = h // 2, h % 2
-            half_chunk(accs, c, w, stat_scr, bins_scr, turn_scr)
-
-            @pl.when(h == 1)
+    def all_chunks(*accs):
+        def step(c, carry):
+            sum_chunk(accs, c, stat_scr, bins_scr, turn_scr)
+
+            @pl.when(c == 0)
             def _():
                 pl.semaphore_wait(barrier, len(greeted))
 
-            @pl.when(w == 1)
+            @pl.when(c > 0)
             def _():
-                turn_chunk(c, turn_scr, hist)
-
-            @pl.when((w == 1) & (c < 3))
+                start_x(c - 1)
+
+            turn_chunk(c, turn_scr, hist)
+
+            @pl.when(c < 3)
             def _():
                 core_copy(c).start()
 
-            @pl.when((w == 1) & (c == 3))
+            @pl.when(c == 3)
             def _():
                 for u in range(2):
                     last_core_copy(u).start()
 
-            @pl.when(((w == 1) & (c >= 1) & (c < 3)) | (h == 6))
-            def _():
-                start_x(c - 1)
-
             return carry
 
-        lax.fori_loop(0, 8, step, 0)
-
-    pl.run_scoped(all_halves, *[pltpu.ACC(q % 2)((16, TILE), F32) for q in range(PAIRS)])
+        lax.fori_loop(0, 4, step, 0)
+
+    pl.run_scoped(all_chunks, *[pltpu.ACC(q % 2)((16, TILE), F32) for q in range(PAIRS)])
 
     start_z(0)
     for u in range(2):

time: 42.4 us -> 42 us (level)
  Pallas kernels: 41.7 us -> 41.2 us
    pallas_call x1, Pallas kernels: 40.5 us -> 40.1 us  [body(): pl.pallas_call(kernel, out_shape=(jax.ShapeDtypeStruct((8, 128), F32), ja...]
where the time goes in v11:
time: 42 us; the launch traced here: 41.9 us
  Pallas kernels  41.2 us (98%)
  between operations  0.64 us (2%)
    pallas_call x1, Pallas kernels, body(): pl.pallas_call(kernel, out_shape=(jax.ShapeDtypeStruct((8, 128), F32), ja...  40.1 us
    pallas_call x1, Pallas kernels, body(): pl.pallas_call(write_kernel, out_shape=(jax.ShapeDtypeStruct((8, 128), F3...  1.12 us

profile of v11, /device:TPU:1, one launch (start us, length us, event | category | flops | bytes accessed | tf_op | source)
XLA Modules:
  0.0 41.9 jit_solution(17340233993016709051)
XLA Ops:
  0.6 40.1 %shard_map.68 = (f32[8,128]{1,0:T(8,128)S(1)}, f32[1,128]{1,0:T(1,128)S(1)}) custom-call(s32[2048,128]{1,0:T(8,128)} %bins_hbm.1, s32[16,128]{1,0:T(8,128)} %bitcast.5, s32[16,128]{1,0:T(8,128)} %bitcast.6, bf16[16,128]{1,0:T(8,128)(2,1)} %bitcast.7, bf16[16,128]{1,0:T(8,128)(2,1)} %bitcast.8), custom_call_target="tpu_custom_call" | custom-call | tf_op jit(solution)/shard_map/pallas_call | solution.py:331
  40.7 1.1 %shard_map.69 = (f32[8,128]{1,0:T(8,128)}, f32[4]{0:T(128)}) custom-call(f32[8,128]{1,0:T(8,128)S(1)} %get-tuple-element.6.gain_ref, f32[1,128]{1,0:T(1,128)S(1)} %get-tuple-element.7.top_ref), custom_call_target="tpu_custom_call" | custom-call | tf_op jit(solution)/shard_map/pallas_call | solution.py:361

commit v12 on v11

--- a/solution.py
+++ b/solution.py
@@ -178,6 +178,12 @@
             core_sum.at[c, :, lax.rem(x + d, NX)], x_in.at[c, d - 1], x_send.at[c, d - 1], x_recv.at[c, d - 1], x_peer[d]
         )
 
+    def near_x_copy(u, d):
+        k = 2 + u
+        return copy(
+            core_sum.at[2, u, lax.rem(x + d, NX)], x_in.at[2, d - 1, u], x_send.at[k, d - 1], x_recv.at[k, d - 1], x_peer[d]
+        )
+
     def z_copy(c, u):
         d = 3 - c if u else 4 + c
         return copy(x_sum.at[c, u], z_in.at[d - 1], z_send.at[d - 1], z_recv.at[d - 1], at(0, d, core))
@@ -208,6 +214,19 @@
         for u in range(2):
             z_copy(c, u).start()
 
+    def start_near_x():
+        add_core(2)
+        for u in range(2):
+            for d in (2, 1, 3):
+                near_x_copy(u, d).start()
+
+    def start_near_z():
+        for u in range(2):
+            for d in (1, 3, 2):
+                near_x_copy(u, d).wait_recv()
+            x_sum[2, u] = core_sum[2, u, x] + x_in[2, 0, u] + x_in[2, 1, u] + x_in[2, 2, u]
+            z_copy(2, u).start()
+
     def all_chunks(*accs):
         def step(c, carry):
             sum_chunk(accs, c, stat_scr, bins_scr, turn_scr)
@@ -216,9 +235,13 @@
             def _():
                 pl.semaphore_wait(barrier, len(greeted))
 
-            @pl.when(c > 0)
+            @pl.when((c > 0) & (c < 3))
             def _():
                 start_x(c - 1)
+
+            @pl.when(c == 3)
+            def _():
+                start_near_x()
 
             turn_chunk(c, turn_scr, hist)
 
@@ -246,8 +269,8 @@
                 last_z_copy(d).start()
             elif d:
                 last_x_copy(d).start()
-    for c in range(1, 3):
-        start_z(c)
+    start_z(1)
+    start_near_z()
     block = core_sum[3, 1, x]
     for c in range(2):
         for u in range(2):
@@ -272,7 +295,11 @@
         for c in range(3):
             core_copy(c).wait_send()
             for d in range(1, NX):
-                x_copy(c, d).wait_send()
+                if c < 2:
+                    x_copy(c, d).wait_send()
+                else:
+                    for u in range(2):
+                        near_x_copy(u, d).wait_send()
             for u in range(2):
                 z_copy(c, u).wait_send()
         for d in range(NX):
@@ -352,7 +379,7 @@
             pltpu.VMEM((NX,) + block, F32),
             pltpu.VMEM((4, 1, 128), F32),
             pltpu.VMEM((4, 7, 1, 128), F32),
-            dma((8,)), dma((5,)), dma((5,)), dma((3, 3)), dma((3, 3)), dma((6,)), dma((6,)),
+            dma((8,)), dma((5,)), dma((5,)), dma((4, 3)), dma((4, 3)), dma((6,)), dma((6,)),
             dma((3,)), dma((3,)), dma((4,)), dma((4,)), dma((4, 7)), dma((4, 7)),
         ],
         compiler_params=pltpu.CompilerParams(collective_id=0, has_side_effects=True, vmem_limit_bytes=24 << 20),

time: 42 us -> 41.9 us (level)
  no operation moved by 1% of the time
where the time goes in v12:
time: 41.9 us; the launch traced here: 41.4 us
  Pallas kernels  40.8 us (97%)
  between operations  0.64 us (2%)
    pallas_call x1, Pallas kernels, body(): pl.pallas_call(kernel, out_shape=(jax.ShapeDtypeStruct((8, 128), F32), ja...  39.7 us
    pallas_call x1, Pallas kernels, body(): pl.pallas_call(write_kernel, out_shape=(jax.ShapeDtypeStruct((8, 128), F3...  1.12 us

profile of v12, /device:TPU:1, one launch (start us, length us, event | category | flops | bytes accessed | tf_op | source)
XLA Modules:
  0.0 41.4 jit_solution(11778038418657588394)
XLA Ops:
  0.6 39.7 %shard_map.68 = (f32[8,128]{1,0:T(8,128)S(1)}, f32[1,128]{1,0:T(1,128)S(1)}) custom-call(s32[2048,128]{1,0:T(8,128)} %bins_hbm.1, s32[16,128]{1,0:T(8,128)} %bitcast.5, s32[16,128]{1,0:T(8,128)} %bitcast.6, bf16[16,128]{1,0:T(8,128)(2,1)} %bitcast.7, bf16[16,128]{1,0:T(8,128)(2,1)} %bitcast.8), custom_call_target="tpu_custom_call" | custom-call | tf_op jit(solution)/shard_map/pallas_call | solution.py:358
  40.3 1.1 %shard_map.69 = (f32[8,128]{1,0:T(8,128)}, f32[4]{0:T(128)}) custom-call(f32[8,128]{1,0:T(8,128)S(1)} %get-tuple-element.6.gain_ref, f32[1,128]{1,0:T(1,128)S(1)} %get-tuple-element.7.top_ref), custom_call_target="tpu_custom_call" | custom-call | tf_op jit(solution)/shard_map/pallas_call | solution.py:388

commit v13 on v11

--- a/solution.py
+++ b/solution.py
@@ -216,10 +216,6 @@
             def _():
                 pl.semaphore_wait(barrier, len(greeted))
 
-            @pl.when(c > 0)
-            def _():
-                start_x(c - 1)
-
             turn_chunk(c, turn_scr, hist)
 
             @pl.when(c < 3)
@@ -230,6 +226,10 @@
             def _():
                 for u in range(2):
                     last_core_copy(u).start()
+
+            @pl.when(c > 0)
+            def _():
+                start_x(c - 1)
 
             return carry
 

time: 42 us -> 42.1 us (level)
  no operation moved by 1% of the time
where the time goes in v13:
time: 42.1 us; the launch traced here: 41.9 us
  Pallas kernels  41.3 us (98%)
  between operations  0.64 us (2%)
    pallas_call x1, Pallas kernels, body(): pl.pallas_call(kernel, out_shape=(jax.ShapeDtypeStruct((8, 128), F32), ja...  40.2 us
    pallas_call x1, Pallas kernels, body(): pl.pallas_call(write_kernel, out_shape=(jax.ShapeDtypeStruct((8, 128), F3...  1.12 us

profile of v13, /device:TPU:1, one launch (start us, length us, event | category | flops | bytes accessed | tf_op | source)
XLA Modules:
  0.0 41.9 jit_solution(8259282116584129391)
XLA Ops:
  0.6 40.2 %shard_map.68 = (f32[8,128]{1,0:T(8,128)S(1)}, f32[1,128]{1,0:T(1,128)S(1)}) custom-call(s32[2048,128]{1,0:T(8,128)} %bins_hbm.1, s32[16,128]{1,0:T(8,128)} %bitcast.5, s32[16,128]{1,0:T(8,128)} %bitcast.6, bf16[16,128]{1,0:T(8,128)(2,1)} %bitcast.7, bf16[16,128]{1,0:T(8,128)(2,1)} %bitcast.8), custom_call_target="tpu_custom_call" | custom-call | tf_op jit(solution)/shard_map/pallas_call | solution.py:331
  40.8 1.1 %shard_map.69 = (f32[8,128]{1,0:T(8,128)}, f32[4]{0:T(128)}) custom-call(f32[8,128]{1,0:T(8,128)S(1)} %get-tuple-element.6.gain_ref, f32[1,128]{1,0:T(1,128)S(1)} %get-tuple-element.7.top_ref), custom_call_target="tpu_custom_call" | custom-call | tf_op jit(solution)/shard_map/pallas_call | solution.py:361

commit v14 on v11

--- a/solution.py
+++ b/solution.py
@@ -212,17 +212,22 @@
         def step(c, carry):
             sum_chunk(accs, c, stat_scr, bins_scr, turn_scr)
 
-            @pl.when(c == 0)
+            @pl.when(c == 1)
             def _():
                 pl.semaphore_wait(barrier, len(greeted))
-
-            @pl.when(c > 0)
+                core_copy(0).start()
+
+            @pl.when(c == 2)
+            def _():
+                start_x(0)
+
+            @pl.when(c > 1)
             def _():
                 start_x(c - 1)
 
             turn_chunk(c, turn_scr, hist)
 
-            @pl.when(c < 3)
+            @pl.when((c == 1) | (c == 2))
             def _():
                 core_copy(c).start()
 

time: 42 us -> 42.7 us (1.017)
  Pallas kernels: 41.2 us -> 42 us
    pallas_call x1, Pallas kernels: 40.1 us -> 40.8 us  [body(): pl.pallas_call(kernel, out_shape=(jax.ShapeDtypeStruct((8, 128), F32), ja...]
where the time goes in v14:
time: 42.7 us; the launch traced here: 42.6 us
  Pallas kernels  42 us (98%)
  between operations  0.64 us (1%)
    pallas_call x1, Pallas kernels, body(): pl.pallas_call(kernel, out_shape=(jax.ShapeDtypeStruct((8, 128), F32), ja...  40.8 us
    pallas_call x1, Pallas kernels, body(): pl.pallas_call(write_kernel, out_shape=(jax.ShapeDtypeStruct((8, 128), F3...  1.12 us

profile of v14, /device:TPU:1, one launch (start us, length us, event | category | flops | bytes accessed | tf_op | source)
XLA Modules:
  0.0 42.6 jit_solution(10999516643081260377)
XLA Ops:
  0.6 40.8 %shard_map.68 = (f32[8,128]{1,0:T(8,128)S(1)}, f32[1,128]{1,0:T(1,128)S(1)}) custom-call(s32[2048,128]{1,0:T(8,128)} %bins_hbm.1, s32[16,128]{1,0:T(8,128)} %bitcast.5, s32[16,128]{1,0:T(8,128)} %bitcast.6, bf16[16,128]{1,0:T(8,128)(2,1)} %bitcast.7, bf16[16,128]{1,0:T(8,128)(2,1)} %bitcast.8), custom_call_target="tpu_custom_call" | custom-call | tf_op jit(solution)/shard_map/pallas_call | solution.py:336
  41.5 1.1 %shard_map.69 = (f32[8,128]{1,0:T(8,128)}, f32[4]{0:T(128)}) custom-call(f32[8,128]{1,0:T(8,128)S(1)} %get-tuple-element.6.gain_ref, f32[1,128]{1,0:T(1,128)S(1)} %get-tuple-element.7.top_ref), custom_call_target="tpu_custom_call" | custom-call | tf_op jit(solution)/shard_map/pallas_call | solution.py:366
